TPU v7x, 32 devices: a whole 2x2x4 slice. The times are simulated.
32 devices in a mesh: grp: 2 (over y), ta: 16 (over z, x, core).
Axes of the slice: x: 2, y: 2, z: 4, core: 2. Of those that a mesh axis runs over, the one named last changes fastest.
Arguments:
- perambulator: bfloat16 [2, 16, 768, 2, 512], P('grp', None, 'ta'), parts along dimension 0, may hold values from -1.1953125 to 1.1953125
- batch_columns: int32 [32], P(('grp', 'ta')), parts along dimension 0, may hold values from 1 to 48, 512 in all
- sink_operator: int32 [2, 16], replicated, may hold values from 0 to 1
- sink_elemental: bfloat16 [8, 16, 2, 128, 128], P('grp'), parts along dimension 0, may hold values from -0.375 to 0.375
- source_elemental: bfloat16 [2, 2, 128, 128], P('grp'), parts along dimension 0, may hold values from -0.375 to 0.375
Outputs:
- loops: bfloat16 [32, 2, 512, 512], P(('grp', 'ta')), parts along dimension 0
There are 2 independent parts, one for each index of `grp`. A program takes and returns all parts, laid end to end along the dimension named above; an argument that names none is the same for every part. Nothing has to cross between parts.
Inputs may be any that keep to these rules, and one draw needn't show every extreme that they name: Batch d holds columns starts[d] to starts[d] + batch_columns[d] - 1 of every source and sink time, in order, in its first batch_columns[d] slots; later slots hold nothing that is read. The entries sum to 512 and the largest equals 48.
All inputs are finite; a program needn't handle non-finite values. No bound on the sum of `batch_columns` on one device may be relied on, other than what follows from the above.
Results may differ from a plain program's by a relative error of at most 0.0057.
Values may be sent and summed in bfloat16 or wider, within the bound.
No kernel may reach another device: no remote copies, remote signals or barrier semaphores. Data moves between devices by JAX's collectives and lax.ppermute only.
A program may use at most 64 MiB of HBM per device.

v0:
```python
import functools

import jax
import jax.numpy as jnp
from jax import lax
from jax.experimental import pallas as pl
from jax.experimental.pallas import tpu as pltpu
from jax.sharding import PartitionSpec as P

NDISP = 2
SPINS = 4
LARGEST_EXCHANGE = 32
LEAD = 2

f32 = jnp.float32
bf16 = jnp.bfloat16

SMEM = pl.BlockSpec(memory_space=pltpu.SMEM)
VMEM = pl.BlockSpec(memory_space=pltpu.VMEM)
HBM = pl.BlockSpec(memory_space=pltpu.HBM)


def matmul(left, right):
    return jnp.dot(left, right, preferred_element_type=f32)


def operators_kernel(tallies, sink, source, own, *refs):
    counts, (f_ref, e_ref, own_ref, told_ref) = refs[:tallies], refs[tallies:]
    own_ref[...] = own[...]
    for number, count in enumerate(counts):
        told_ref[number] = jnp.full(told_ref.shape[1:], count[0], jnp.int32).astype(f32)
    n = sink.shape[-1]
    row = lax.broadcasted_iota(jnp.int32, (2 * n, 2 * n), 0)
    col = lax.broadcasted_iota(jnp.int32, (2 * n, 2 * n), 1)
    spread = jnp.where(col == (row % 2) * n + row // 2, 1.0, 0.0).astype(bf16)
    gathered = jnp.where(row == (col % 2) * n + col // 2, 1.0, 0.0).astype(bf16)
    f_real, f_imag = source[0], source[1]
    stacked = (
        jnp.concatenate([jnp.concatenate([f_real, f_imag], 1), jnp.concatenate([-f_imag, f_real], 1)], 0),
        jnp.concatenate([jnp.concatenate([f_imag, -f_real], 1), jnp.concatenate([f_real, f_imag], 1)], 0),
    )
    for part in range(2):
        rows = matmul(spread, stacked[part]).astype(bf16)
        f_ref[2 * n * part : 2 * n * (part + 1), :] = matmul(rows, gathered).astype(bf16)
    e_real, e_imag = sink[0], sink[1]
    e_ref[:n, :n] = e_real
    e_ref[:n, n:] = -e_imag
    e_ref[n:, :n] = e_imag
    e_ref[n:, n:] = e_real


def operators(sink, source, own, counts):
    n = source.shape[-1]
    return pl.pallas_call(
        functools.partial(operators_kernel, len(counts)),
        out_shape=(
            jax.ShapeDtypeStruct((4 * n, 2 * n), bf16),
            jax.ShapeDtypeStruct((2 * n, 2 * n), bf16),
            jax.ShapeDtypeStruct(own.shape, bf16),
            jax.ShapeDtypeStruct((max(len(counts), 1), 8, 128), f32),
        ),
        in_specs=[VMEM] * 3 + [SMEM] * len(counts),
        out_specs=[VMEM] * 4,
        cost_estimate=pl.CostEstimate(flops=10**8, bytes_accessed=10**6, transcendentals=0),
        compiler_params=pltpu.CompilerParams(vmem_limit_bytes=8 * 2**20),
        name="operators",
    )(sink, source, own, *counts)


def cut_kernel(steps, count_hbm, operator_hbm, columns_ref, sink_ref, source_ref, *refs):
    blocks, refs = refs[: len(steps)], refs[len(steps) :]
    sink, source, count_ref, operator_ref, count_sem, operator_sem, pair_sems, sems = refs
    rank = lax.axis_index("ta")
    sinks = sink_ref.shape[1]
    source_index, sink_index = rank // sinks, rank % sinks
    operator = pltpu.make_async_copy(operator_hbm, operator_ref, operator_sem)
    operator.start()
    copies = [pltpu.make_async_copy(count_hbm, count_ref, count_sem)]
    for number, (step, block) in enumerate(zip(steps, blocks)):
        copies.append(pltpu.make_async_copy(columns_ref.at[rank ^ step_mask(step, rank)], block.at[0], sems.at[number]))
    copies.append(pltpu.make_async_copy(source_ref.at[source_index], source, pair_sems.at[0]))
    for copy in copies:
        copy.start()
    operator.wait()
    chosen = operator_ref[0, sink_index] * NDISP + operator_ref[1, sink_index]
    copies.append(pltpu.make_async_copy(sink_ref.at[chosen, sink_index], sink, pair_sems.at[1]))
    copies[-1].start()
    for copy in copies:
        copy.wait()
    if not blocks:
        return
    count = count_ref[0]
    _, capacity, parts, order = blocks[0].shape

    @pl.when(count < capacity)
    def _():
        row = lax.broadcasted_iota(jnp.int32, (parts, order), 0)
        mark = jnp.where(row == 0, jnp.inf, count.astype(f32)).astype(bf16)
        for block in blocks:
            block[0, capacity - 1] = mark


def cut_blocks(counts, sink_operator, columns, sink_elemental, source_elemental, steps):
    _, capacity, parts, order = columns.shape
    pair_shape = jax.ShapeDtypeStruct(source_elemental.shape[1:], bf16)
    *blocks, sink, source = pl.pallas_call(
        functools.partial(cut_kernel, steps),
        out_shape=[jax.ShapeDtypeStruct((1, capacity, parts, order), bf16)] * len(steps) + [pair_shape] * 2,
        in_specs=[HBM] * 5,
        out_specs=[VMEM] * (len(steps) + 2),
        scratch_shapes=[
            pltpu.SMEM(counts.shape, jnp.int32),
            pltpu.SMEM(sink_operator.shape, jnp.int32),
            pltpu.SemaphoreType.DMA,
            pltpu.SemaphoreType.DMA,
            pltpu.SemaphoreType.DMA((2,)),
            pltpu.SemaphoreType.DMA((max(len(steps), 1),)),
        ],
        cost_estimate=pl.CostEstimate(flops=0, bytes_accessed=3 * 10**6, transcendentals=0),
        compiler_params=pltpu.CompilerParams(vmem_limit_bytes=60 * 2**20),
        name="cut_blocks",
    )(counts, sink_operator, columns, sink_elemental, source_elemental)
    return blocks, sink, source


def place_blocks(table, sources, arrays, packed):
    spins, _, _, n = packed.shape
    unroll = 8

    def place(array, index, batch):
        count, start = table[0, batch], table[1, batch]

        def one(column, carry):
            value = array[index, column]
            for spin in range(spins):
                packed[spin, start + column] = value[:, n * spin : n * (spin + 1)]
            return carry

        def several(group, carry):
            for column in range(unroll):
                one(group * unroll + column, carry)
            return carry

        whole = count // unroll
        lax.fori_loop(0, whole, several, 0)
        lax.fori_loop(whole * unroll, count, one, 0)

    for array, batch in zip(arrays, sources):
        if batch is None:
            lax.fori_loop(0, array.shape[0], lambda batch, carry, array=array: (place(array, batch, batch), carry)[1], 0)
        else:
            place(array, 0, batch)


def pair_kernel(batches_of, *refs):
    f_ref, e_ref, told_ref, *arrays = refs[:-7]
    out_hbm, packed, turned, right, result, table, sems = refs[-7:]
    spins, order, _, n = packed.shape
    if batches_of is None:
        *arrays, counts = arrays
        sources = [None]
        pltpu.sync_copy(counts, table.at[0])
    else:
        sources = batches_of(lax.axis_index("ta"))
        for number, (batch, array) in enumerate(zip(sources, arrays)):
            _, capacity, _, _ = array.shape
            if 1 <= number <= LEAD:
                told = told_ref[number - 1]
            else:
                last = array[0, capacity - 1, :, :128].astype(f32)
                told = jnp.where(last[:1] == jnp.inf, last[1:], float(capacity))
            table[0, batch] = told[0, 0].astype(jnp.int32)

    def running(batch, start):
        table[1, batch] = start
        return start + table[0, batch]

    lax.fori_loop(0, table.shape[1], running, jnp.int32(0))
    place_blocks(table, sources, arrays, packed)
    rows = packed.reshape(spins, 2 * order, n)
    half, per_half = order // 2, spins // 2
    for spin in range(spins):
        turned[n * spin : n * (spin + 1), :] = rows[spin].T
    copies = []
    for side in range(2):
        mine = slice(half * side, half * (side + 1))
        for spin in range(spins):
            near = slice(2 * n * spin, 2 * n * (spin + 1))
            column = jnp.concatenate([rows[per_half * side + k, near, :] for k in range(per_half)], axis=1)
            product = matmul(f_ref[...], column).astype(bf16)
            right[side, near, :half] = product[: 2 * n]
            right[side, near, half:] = product[2 * n :]
        total = matmul(turned[...], right[side]).astype(bf16)
        for spin in range(spins):
            here = slice(n * spin, n * (spin + 1))
            middle = jnp.concatenate([total[here, :half], total[here, half:]], axis=0)
            outcome = matmul(e_ref[...], middle)
            if (spin < per_half) != (side == 0):
                outcome = -outcome
            for part in range(2):
                result[part, here, mine] = outcome[n * part : n * (part + 1)].astype(bf16)
        copies.append(pltpu.make_async_copy(result.at[:, :, mine], out_hbm.at[:, :, mine], sems.at[side]))
        copies[-1].start()
    for copy in copies:
        copy.wait()


def pair_loop(batches_of, arrays, f_matrix, e_matrix, told, batches, order):
    n = order // SPINS
    return pl.pallas_call(
        functools.partial(pair_kernel, batches_of),
        out_shape=jax.ShapeDtypeStruct((2, order, order), bf16),
        in_specs=[VMEM] * (len(arrays) + 3),
        out_specs=HBM,
        scratch_shapes=[
            pltpu.VMEM((SPINS, order, 2, n), bf16),
            pltpu.VMEM((order, 2 * order), bf16),
            pltpu.VMEM((2, 2 * order, order), bf16),
            pltpu.VMEM((2, order, order), bf16),
            pltpu.SMEM((2, batches), jnp.int32),
            pltpu.SemaphoreType.DMA((2,)),
        ],
        cost_estimate=pl.CostEstimate(flops=2 * 10**9, bytes_accessed=3 * 10**6, transcendentals=0),
        compiler_params=pltpu.CompilerParams(vmem_limit_bytes=24 * 2**20),
        name="pair_loop",
    )(f_matrix, e_matrix, told, *arrays)


OWN = (0, 0, 1)


def exchange_steps(devices):
    far, near, low = list(range(devices // 2, devices)), [], devices // 4
    while low > 1:
        near += range(low, 2 * low)
        low //= 2
    steps = [(far[0], far[0], 1)]
    for number, (a, b) in enumerate(zip(far[1:-1], near)):
        classes = [c for c in range(1, devices) if parity(c & a) == 0 and parity(c & b) == 0]
        c = max(classes, key=lambda c: (c & 1, -bin(c).count("1"), c))
        steps += [(a, b, c), (b, a, c)]
        if number == devices // 4 - 1:
            steps.append((1, 1, 1))
    return steps + [(far[-1], far[-1], 1)]


def parity(value):
    return bin(value).count("1") % 2


def step_mask(step, rank):
    even, odd, class_mask = step
    if even == odd:
        return even
    folded, bit = 0, 0
    while class_mask >> bit:
        if class_mask >> bit & 1:
            folded = folded ^ (rank >> bit)
        bit += 1
    return jnp.where(folded & 1 == 0, even, odd)


def step_pairs(step, devices):
    even, odd, class_mask = step
    return [(i, i ^ (odd if parity(i & class_mask) else even)) for i in range(devices)]


def exchange(outgoing, counts, rank, cut):
    devices = outgoing.shape[0]
    steps = exchange_steps(devices)
    blocks = [lax.dynamic_slice_in_dim(outgoing, rank ^ step_mask(step, rank), 1) for step in steps[:LEAD]]
    (own, *others), sink, source = cut([OWN] + steps[LEAD:])
    tallies = []
    for step in steps[:LEAD]:
        tallies.append(lax.ppermute(counts, "ta", step_pairs(step, devices)))
    received = []
    for step, block in zip(steps, blocks + others):
        received.append(lax.ppermute(block, "ta", step_pairs(step, devices)))
    f_matrix, e_matrix, own, told = operators(sink, source, own, tallies)
    return [own] + received, f_matrix, e_matrix, told, lambda me: [me ^ step_mask(step, me) for step in [OWN] + steps]


def local(perambulator, batch_columns, sink_operator, sink_elemental, source_elemental):
    source_count, sink_count, capacity, parts, order = perambulator.shape
    devices = lax.axis_size("ta")
    assert source_count * sink_count == devices
    rank = lax.axis_index("ta").astype(jnp.int32)
    outgoing = perambulator.reshape(devices, capacity, parts, order)
    cut = functools.partial(cut_blocks, batch_columns, sink_operator, outgoing, sink_elemental, source_elemental)
    if exchanged(devices):
        arrays, f_matrix, e_matrix, told, batches_of = exchange(outgoing, batch_columns, rank, cut)
    else:
        _, sink, source = cut([])
        arrays = [lax.all_to_all(outgoing, "ta", split_axis=0, concat_axis=0, tiled=True)]
        arrays.append(lax.all_gather(batch_columns, "ta", axis=0, tiled=True))
        f_matrix, e_matrix, _, told = operators(sink, source, sink, [])
        batches_of = None
    return pair_loop(batches_of, arrays, f_matrix, e_matrix, told, devices, order)[None]


def exchanged(devices):
    return 8 <= devices <= LARGEST_EXCHANGE and devices & (devices - 1) == 0


def solution(mesh):
    placed = (
        P("grp", None, "ta", None, None),
        P(("grp", "ta")),
        P(),
        P("grp", None, None, None, None),
        P("grp", None, None, None),
    )
    return jax.shard_map(
        local,
        mesh=mesh,
        in_specs=placed,
        out_specs=P(("grp", "ta"), None, None, None),
        check_vma=False,
    )
```

profile of v0, /device:TPU:9, one launch (start us, length us, event | category | flops | bytes accessed | tf_op | source)
XLA Modules:
  0.0 48.4 jit_solution(1954284690130600478)
XLA Ops:
  0.0 0.0 collective-permute-start.1
  0.0 2.9 %collective-permute-start = (s32[1]{0:T(128)}, s32[1]{0:T(128)}, u32[]{:S(2)}, u32[]{:S(2)}) collective-permute-start(s32[1]{0:T(128)} %param.6), channel_id=1, source_target_pairs={{0,8},{1,9},{2,10},{3,11},{4,12},{5,13},{6,14},{7,15},{8,0},{9,1},... | collective-permute-start | bytes 20 | tf_op jit(solution)/shard_map/ppermute | solution.py:275
  2.9 1.1 %dynamic-slice_bitcast_fusion = (bf16[1,48,2,512]{3,2,1,0:T(2,128)(2,1)S(1)}, bf16[1,48,2,512]{3,2,1,0:T(2,128)(2,1)S(1)}) fusion(bf16[1,16,48,2,512]{4,3,2,1,0:T(2,128)(2,1)} %param.5, s32[]{:T(128)S(6)} %select_n.12, s32[]{:T(128)S(6)} %select_n.10), kind=kLoop, calls=%fused_computation | loop fusion | bytes 393224 | tf_op jit(solution)/shard_map/dynamic_slice | solution.py:271
  4.0 0.1 collective-permute-start.3
  4.1 3.0 %collective-permute-start.2 = (bf16[1,48,2,512]{3,2,1,0:T(2,128)(2,1)S(1)}, bf16[1,48,2,512]{3,2,1,0:T(2,128)(2,1)S(1)}, u32[]{:S(2)}, u32[]{:S(2)}) collective-permute-start(bf16[1,48,2,512]{3,2,1,0:T(2,128)(2,1)S(1)} %get-tuple-element.46), channel_id=1, source_target_pairs={{0,8},{1,9},{2,10},{3,11},{4,12},{5,13},{6,14},{7,15},{8,0},{9,1},... | collective-permute-start | bytes 294920 | tf_op jit(solution)/shard_map/ppermute | solution.py:278
  7.8 3.1 %cut_blocks.1 = (bf16[1,48,2,512]{3,2,1,0:T(2,128)(2,1)}, bf16[1,48,2,512]{3,2,1,0:T(2,128)(2,1)}, bf16[1,48,2,512]{3,2,1,0:T(2,128)(2,1)}, bf16[1,48,2,512]{3,2...) custom-call(s32[1]{0:T(128)S(6)} %copy.6.count_hbm, ...), custom_call_target="tpu_custom_call" | custom-call | bytes 3000000 | tf_op jit(solution)/shard_map/cut_blocks/pallas_call | solution.py:106
  10.9 0.4 collective-permute-start.4
  11.3 0.0 collective-permute-done.1.refs_1_
  11.3 1.9 %collective-permute-start.5 = (bf16[1,48,2,512]{3,2,1,0:T(2,128)(2,1)}, bf16[1,48,2,512]{3,2,1,0:T(2,128)(2,1)S(1)}, u32[]{:S(2)}, u32[]{:S(2)}) collective-permute-start(bf16[1,48,2,512]{3,2,1,0:T(2,128)(2,1)} %get-tuple-element.33), channel_id=1, source_target_pairs={{0,10},{1,4},{2,8},{3,6},{4,1},{5,15},{6,3},{7,13},{8,2},{9,12},{1... | collective-permute-start | bytes 294920 | tf_op jit(solution)/shard_map/ppermute | solution.py:278
  13.2 0.0 collective-permute-done.refs_0_
  13.2 2.9 %collective-permute-start.6 = (bf16[1,48,2,512]{3,2,1,0:T(2,128)(2,1)}, bf16[1,48,2,512]{3,2,1,0:T(2,128)(2,1)S(1)}, u32[]{:S(2)}, u32[]{:S(2)}) collective-permute-start(bf16[1,48,2,512]{3,2,1,0:T(2,128)(2,1)} %get-tuple-element.34), channel_id=1, source_target_pairs={{0,5},{1,11},{2,7},{3,9},{4,14},{5,0},{6,12},{7,2},{8,13},{9,3},{1... | collective-permute-start | bytes 294920 | tf_op jit(solution)/shard_map/ppermute | solution.py:278
  16.1 0.0 collective-permute-done.3.refs_5_
  16.1 0.0 collective-permute-start.7
  16.1 0.0 collective-permute-done.2.refs_4_
  16.1 1.4 %collective-permute-start.8 = (bf16[1,48,2,512]{3,2,1,0:T(2,128)(2,1)}, bf16[1,48,2,512]{3,2,1,0:T(2,128)(2,1)S(1)}, u32[]{:S(2)}, u32[]{:S(2)}) collective-permute-start(bf16[1,48,2,512]{3,2,1,0:T(2,128)(2,1)} %get-tuple-element.36), channel_id=1, source_target_pairs={{0,6},{1,10},{2,4},{3,8},{4,2},{5,14},{6,0},{7,12},{8,3},{9,15},{1... | collective-permute-start | bytes 294920 | tf_op jit(solution)/shard_map/ppermute | solution.py:278
  17.6 0.0 collective-permute-done.4.refs_6_
  17.6 1.6 %collective-permute-start.9 = (bf16[1,48,2,512]{3,2,1,0:T(2,128)(2,1)}, bf16[1,48,2,512]{3,2,1,0:T(2,128)(2,1)S(1)}, u32[]{:S(2)}, u32[]{:S(2)}) collective-permute-start(bf16[1,48,2,512]{3,2,1,0:T(2,128)(2,1)} %get-tuple-element.37), channel_id=1, source_target_pairs={{0,12},{1,6},{2,5},{3,15},{4,8},{5,2},{6,1},{7,11},{8,4},{9,14},{1... | collective-permute-start | bytes 294920 | tf_op jit(solution)/shard_map/ppermute | solution.py:278
  19.2 0.0 collective-permute-done.5.refs_7_
  19.2 0.8 %collective-permute-start.10 = (bf16[1,48,2,512]{3,2,1,0:T(2,128)(2,1)}, bf16[1,48,2,512]{3,2,1,0:T(2,128)(2,1)S(1)}, u32[]{:S(2)}, u32[]{:S(2)}) collective-permute-start(bf16[1,48,2,512]{3,2,1,0:T(2,128)(2,1)} %get-tuple-element.38), channel_id=1, source_target_pairs={{0,7},{1,13},{2,14},{3,4},{4,3},{5,9},{6,10},{7,0},{8,15},{9,5},{1... | collective-permute-start | bytes 294920 | tf_op jit(solution)/shard_map/ppermute | solution.py:278
  20.0 2.1 %collective-permute-done.6.refs_8_ = bf16[1,48,2,512]{3,2,1,0:T(2,128)(2,1)S(1)} collective-permute-done((bf16[1,48,2,512]{3,2,1,0:T(2,128)(2,1)}, bf16[1,48,2,512]{3,2,1,0:T(2,128)(2,1)S(1)}, u32[]{:S(2)}, u32[]{:S(2)}) %collective-permute-start.6) | collective-permute-done | bytes 98336 | tf_op jit(solution)/shard_map/ppermute | solution.py:278
  22.1 1.8 %collective-permute-start.11 = (bf16[1,48,2,512]{3,2,1,0:T(2,128)(2,1)}, bf16[1,48,2,512]{3,2,1,0:T(2,128)(2,1)S(1)}, u32[]{:S(2)}, u32[]{:S(2)}) collective-permute-start(bf16[1,48,2,512]{3,2,1,0:T(2,128)(2,1)} %get-tuple-element.39), channel_id=1, source_target_pairs={{0,1},{1,0},{2,3},{3,2},{4,5},{5,4},{6,7},{7,6},{8,9},{9,8},{10,11... | collective-permute-start | bytes 294920 | tf_op jit(solution)/shard_map/ppermute | solution.py:278
  23.9 0.0 collective-permute-done.7.refs_9_
  23.9 3.3 %collective-permute-start.12 = (bf16[1,48,2,512]{3,2,1,0:T(2,128)(2,1)}, bf16[1,48,2,512]{3,2,1,0:T(2,128)(2,1)S(1)}, u32[]{:S(2)}, u32[]{:S(2)}) collective-permute-start(bf16[1,48,2,512]{3,2,1,0:T(2,128)(2,1)} %get-tuple-element.40), channel_id=1, source_target_pairs={{0,13},{1,3},{2,15},{3,1},{4,9},{5,7},{6,11},{7,5},{8,10},{9,4},{1... | collective-permute-start | bytes 294920 | tf_op jit(solution)/shard_map/ppermute | solution.py:278
  27.2 0.0 collective-permute-done.8.refs_10_
  27.2 0.5 collective-permute-start.13
  27.7 1.1 %collective-permute-done.9.refs_11_ = bf16[1,48,2,512]{3,2,1,0:T(2,128)(2,1)S(1)} collective-permute-done((bf16[1,48,2,512]{3,2,1,0:T(2,128)(2,1)}, bf16[1,48,2,512]{3,2,1,0:T(2,128)(2,1)S(1)}, u32[]{:S(2)}, u32[]{:S(2)}) %collective-permute-start.9) | collective-permute-done | bytes 98336 | tf_op jit(solution)/shard_map/ppermute | solution.py:278
  28.8 0.0 collective-permute-start.14
  28.8 0.7 %collective-permute-done.10.refs_12_ = bf16[1,48,2,512]{3,2,1,0:T(2,128)(2,1)S(1)} collective-permute-done((bf16[1,48,2,512]{3,2,1,0:T(2,128)(2,1)}, bf16[1,48,2,512]{3,2,1,0:T(2,128)(2,1)S(1)}, u32[]{:S(2)}, u32[]{:S(2)}) %collective-permute-start.10) | collective-permute-done | bytes 98336 | tf_op jit(solution)/shard_map/ppermute | solution.py:278
  29.5 3.2 %collective-permute-start.15 = (bf16[1,48,2,512]{3,2,1,0:T(2,128)(2,1)}, bf16[1,48,2,512]{3,2,1,0:T(2,128)(2,1)S(1)}, u32[]{:S(2)}, u32[]{:S(2)}) collective-permute-start(bf16[1,48,2,512]{3,2,1,0:T(2,128)(2,1)} %get-tuple-element.43), channel_id=1, source_target_pairs={{0,3},{1,15},{2,12},{3,0},{4,7},{5,11},{6,8},{7,4},{8,6},{9,10},{1... | collective-permute-start | bytes 294920 | tf_op jit(solution)/shard_map/ppermute | solution.py:278
  32.6 0.0 collective-permute-done.11.refs_13_
  32.6 2.2 %collective-permute-start.16 = (bf16[1,48,2,512]{3,2,1,0:T(2,128)(2,1)}, bf16[1,48,2,512]{3,2,1,0:T(2,128)(2,1)S(1)}, u32[]{:S(2)}, u32[]{:S(2)}) collective-permute-start(bf16[1,48,2,512]{3,2,1,0:T(2,128)(2,1)} %get-tuple-element.44), channel_id=1, source_target_pairs={{0,15},{1,14},{2,13},{3,12},{4,11},{5,10},{6,9},{7,8},{8,7},{9,6},... | collective-permute-start | bytes 294920 | tf_op jit(solution)/shard_map/ppermute | solution.py:278
  34.8 0.0 copy-start
  34.8 0.9 %copy-done = bf16[1,48,2,512]{3,2,1,0:T(2,128)(2,1)S(1)} copy-done((bf16[1,48,2,512]{3,2,1,0:T(2,128)(2,1)S(1)}, bf16[1,48,2,512]{3,2,1,0:T(2,128)(2,1)}, u32[]{:S(2)}) %copy-start) | copy-done | bytes 98328
  35.7 0.0 copy-start.1
  35.7 0.8 %copy-done.1 = bf16[2,128,128]{2,1,0:T(8,128)(2,1)S(1)} copy-done((bf16[2,128,128]{2,1,0:T(8,128)(2,1)S(1)}, bf16[2,128,128]{2,1,0:T(8,128)(2,1)}, u32[]{:S(2)}) %copy-start.1) | copy-done | bytes 65560
  36.5 0.0 copy-start.2
  36.5 0.8 %copy-done.2 = bf16[2,128,128]{2,1,0:T(8,128)(2,1)S(1)} copy-done((bf16[2,128,128]{2,1,0:T(8,128)(2,1)S(1)}, bf16[2,128,128]{2,1,0:T(8,128)(2,1)}, u32[]{:S(2)}) %copy-start.2) | copy-done | bytes 65560
  37.4 1.7 %operators.1 = (bf16[512,256]{1,0:T(8,128)(2,1)S(1)}, bf16[256,256]{1,0:T(8,128)(2,1)S(1)}, bf16[1,48,2,512]{3,2,1,0:T(2,128)(2,1)S(1)}, f32[2,8,128]{2,1,0:T(8,128)S(1)}) custom-call(bf16[2,128,128]{2,1,0:T(8,128)(2,1)S(1)} %copy-done.1, bf16[2,128,128]{2,1,0:T(8,128)(2,1)S(1)} %copy-done.2, bf16[1,48,2,512]{3,2,1,0:T(2,128)(2,1)S(1)} %copy-done, ...), custom_call_target="tpu_custom_call" | custom-call | flops 100000000 | bytes 1000000 | tf_op jit(solution)/shard_map/operators/pallas_call | solution.py:54
  39.1 0.0 collective-permute-done.12.refs_14_
  39.1 0.0 collective-permute-done.13.refs_15_
  39.1 0.0 collective-permute-done.14.refs_16_
  39.1 2.4 %collective-permute-done.15.refs_17_ = bf16[1,48,2,512]{3,2,1,0:T(2,128)(2,1)S(1)} collective-permute-done((bf16[1,48,2,512]{3,2,1,0:T(2,128)(2,1)}, bf16[1,48,2,512]{3,2,1,0:T(2,128)(2,1)S(1)}, u32[]{:S(2)}, u32[]{:S(2)}) %collective-permute-start.15) | collective-permute-done | bytes 98336 | tf_op jit(solution)/shard_map/ppermute | solution.py:278
  41.5 2.1 %collective-permute-done.16.refs_18_ = bf16[1,48,2,512]{3,2,1,0:T(2,128)(2,1)S(1)} collective-permute-done((bf16[1,48,2,512]{3,2,1,0:T(2,128)(2,1)}, bf16[1,48,2,512]{3,2,1,0:T(2,128)(2,1)S(1)}, u32[]{:S(2)}, u32[]{:S(2)}) %collective-permute-start.16) | collective-permute-done | bytes 98336 | tf_op jit(solution)/shard_map/ppermute | solution.py:278
  43.6 4.8 %pair_loop.1 = bf16[2,512,512]{2,1,0:T(8,128)(2,1)} custom-call(bf16[512,256]{1,0:T(8,128)(2,1)S(1)} %get-tuple-element.28.refs_0_, bf16[256,256]{1,0:T(8,128)(2,1)S(1)} %get-tuple-element.29.refs_1_, f32[2,8,128]{2,1,0:T(8,128)S(1)} %get-tuple-element.30.refs_2_, bf16[1,48,2,512]{3,2,1,0:T(2,128)(2,1)S(1)} %get-tuple-element.31.refs_3_, ...), custom_call_target="tpu_custom_call" | custom-call | flops 2000000000 | bytes 3000000 | tf_op jit(solution)/shard_map/pair_loop/pallas_call | solution.py:210
Async XLA Ops:
  0.0 11.3 %collective-permute-start.1 = (s32[1]{0:T(128)}, s32[1]{0:T(128)}, u32[]{:S(2)}, u32[]{:S(2)}) collective-permute-start(s32[1]{0:T(128)} %param.6), channel_id=1, source_target_pairs={{0,9},{1,5},{2,11},{3,7},{4,13},{5,1},{6,15},{7,3},{8,12},{9,0},{1... | collective-permute-start | bytes 20 | tf_op jit(solution)/shard_map/ppermute | solution.py:275
  0.0 13.2 %collective-permute-start = (s32[1]{0:T(128)}, s32[1]{0:T(128)}, u32[]{:S(2)}, u32[]{:S(2)}) collective-permute-start(s32[1]{0:T(128)} %param.6), channel_id=1, source_target_pairs={{0,8},{1,9},{2,10},{3,11},{4,12},{5,13},{6,14},{7,15},{8,0},{9,1},... | collective-permute-start | bytes 20 | tf_op jit(solution)/shard_map/ppermute | solution.py:275
  4.0 12.1 %collective-permute-start.3 = (bf16[1,48,2,512]{3,2,1,0:T(2,128)(2,1)S(1)}, bf16[1,48,2,512]{3,2,1,0:T(2,128)(2,1)S(1)}, u32[]{:S(2)}, u32[]{:S(2)}) collective-permute-start(bf16[1,48,2,512]{3,2,1,0:T(2,128)(2,1)S(1)} %get-tuple-element.45), channel_id=1, source_target_pairs={{0,9},{1,5},{2,11},{3,7},{4,13},{5,1},{6,15},{7,3},{8,12},{9,0},{1... | collective-permute-start | bytes 294920 | tf_op jit(solution)/shard_map/ppermute | solution.py:278
  4.1 12.1 %collective-permute-start.2 = (bf16[1,48,2,512]{3,2,1,0:T(2,128)(2,1)S(1)}, bf16[1,48,2,512]{3,2,1,0:T(2,128)(2,1)S(1)}, u32[]{:S(2)}, u32[]{:S(2)}) collective-permute-start(bf16[1,48,2,512]{3,2,1,0:T(2,128)(2,1)S(1)} %get-tuple-element.46), channel_id=1, source_target_pairs={{0,8},{1,9},{2,10},{3,11},{4,12},{5,13},{6,14},{7,15},{8,0},{9,1},... | collective-permute-start | bytes 294920 | tf_op jit(solution)/shard_map/ppermute | solution.py:278
  10.9 6.7 %collective-permute-start.4 = (bf16[1,48,2,512]{3,2,1,0:T(2,128)(2,1)}, bf16[1,48,2,512]{3,2,1,0:T(2,128)(2,1)S(1)}, u32[]{:S(2)}, u32[]{:S(2)}) collective-permute-start(bf16[1,48,2,512]{3,2,1,0:T(2,128)(2,1)} %get-tuple-element.32), channel_id=1, source_target_pairs={{0,4},{1,8},{2,6},{3,10},{4,0},{5,12},{6,2},{7,14},{8,1},{9,13},{1... | collective-permute-start | bytes 294920 | tf_op jit(solution)/shard_map/ppermute | solution.py:278
  11.3 7.9 %collective-permute-start.5 = (bf16[1,48,2,512]{3,2,1,0:T(2,128)(2,1)}, bf16[1,48,2,512]{3,2,1,0:T(2,128)(2,1)S(1)}, u32[]{:S(2)}, u32[]{:S(2)}) collective-permute-start(bf16[1,48,2,512]{3,2,1,0:T(2,128)(2,1)} %get-tuple-element.33), channel_id=1, source_target_pairs={{0,10},{1,4},{2,8},{3,6},{4,1},{5,15},{6,3},{7,13},{8,2},{9,12},{1... | collective-permute-start | bytes 294920 | tf_op jit(solution)/shard_map/ppermute | solution.py:278
  13.2 8.9 %collective-permute-start.6 = (bf16[1,48,2,512]{3,2,1,0:T(2,128)(2,1)}, bf16[1,48,2,512]{3,2,1,0:T(2,128)(2,1)S(1)}, u32[]{:S(2)}, u32[]{:S(2)}) collective-permute-start(bf16[1,48,2,512]{3,2,1,0:T(2,128)(2,1)} %get-tuple-element.34), channel_id=1, source_target_pairs={{0,5},{1,11},{2,7},{3,9},{4,14},{5,0},{6,12},{7,2},{8,13},{9,3},{1... | collective-permute-start | bytes 294920 | tf_op jit(solution)/shard_map/ppermute | solution.py:278
  16.1 7.8 %collective-permute-start.7 = (bf16[1,48,2,512]{3,2,1,0:T(2,128)(2,1)}, bf16[1,48,2,512]{3,2,1,0:T(2,128)(2,1)S(1)}, u32[]{:S(2)}, u32[]{:S(2)}) collective-permute-start(bf16[1,48,2,512]{3,2,1,0:T(2,128)(2,1)} %get-tuple-element.35), channel_id=1, source_target_pairs={{0,11},{1,7},{2,9},{3,5},{4,15},{5,3},{6,13},{7,1},{8,14},{9,2},{1... | collective-permute-start | bytes 294920 | tf_op jit(solution)/shard_map/ppermute | solution.py:278
  16.1 11.1 %collective-permute-start.8 = (bf16[1,48,2,512]{3,2,1,0:T(2,128)(2,1)}, bf16[1,48,2,512]{3,2,1,0:T(2,128)(2,1)S(1)}, u32[]{:S(2)}, u32[]{:S(2)}) collective-permute-start(bf16[1,48,2,512]{3,2,1,0:T(2,128)(2,1)} %get-tuple-element.36), channel_id=1, source_target_pairs={{0,6},{1,10},{2,4},{3,8},{4,2},{5,14},{6,0},{7,12},{8,3},{9,15},{1... | collective-permute-start | bytes 294920 | tf_op jit(solution)/shard_map/ppermute | solution.py:278
  17.6 11.2 %collective-permute-start.9 = (bf16[1,48,2,512]{3,2,1,0:T(2,128)(2,1)}, bf16[1,48,2,512]{3,2,1,0:T(2,128)(2,1)S(1)}, u32[]{:S(2)}, u32[]{:S(2)}) collective-permute-start(bf16[1,48,2,512]{3,2,1,0:T(2,128)(2,1)} %get-tuple-element.37), channel_id=1, source_target_pairs={{0,12},{1,6},{2,5},{3,15},{4,8},{5,2},{6,1},{7,11},{8,4},{9,14},{1... | collective-permute-start | bytes 294920 | tf_op jit(solution)/shard_map/ppermute | solution.py:278
  19.2 10.3 %collective-permute-start.10 = (bf16[1,48,2,512]{3,2,1,0:T(2,128)(2,1)}, bf16[1,48,2,512]{3,2,1,0:T(2,128)(2,1)S(1)}, u32[]{:S(2)}, u32[]{:S(2)}) collective-permute-start(bf16[1,48,2,512]{3,2,1,0:T(2,128)(2,1)} %get-tuple-element.38), channel_id=1, source_target_pairs={{0,7},{1,13},{2,14},{3,4},{4,3},{5,9},{6,10},{7,0},{8,15},{9,5},{1... | collective-permute-start | bytes 294920 | tf_op jit(solution)/shard_map/ppermute | solution.py:278
  22.1 10.5 %collective-permute-start.11 = (bf16[1,48,2,512]{3,2,1,0:T(2,128)(2,1)}, bf16[1,48,2,512]{3,2,1,0:T(2,128)(2,1)S(1)}, u32[]{:S(2)}, u32[]{:S(2)}) collective-permute-start(bf16[1,48,2,512]{3,2,1,0:T(2,128)(2,1)} %get-tuple-element.39), channel_id=1, source_target_pairs={{0,1},{1,0},{2,3},{3,2},{4,5},{5,4},{6,7},{7,6},{8,9},{9,8},{10,11... | collective-permute-start | bytes 294920 | tf_op jit(solution)/shard_map/ppermute | solution.py:278
  23.9 15.2 %collective-permute-start.12 = (bf16[1,48,2,512]{3,2,1,0:T(2,128)(2,1)}, bf16[1,48,2,512]{3,2,1,0:T(2,128)(2,1)S(1)}, u32[]{:S(2)}, u32[]{:S(2)}) collective-permute-start(bf16[1,48,2,512]{3,2,1,0:T(2,128)(2,1)} %get-tuple-element.40), channel_id=1, source_target_pairs={{0,13},{1,3},{2,15},{3,1},{4,9},{5,7},{6,11},{7,5},{8,10},{9,4},{1... | collective-permute-start | bytes 294920 | tf_op jit(solution)/shard_map/ppermute | solution.py:278
  27.2 11.9 %collective-permute-start.13 = (bf16[1,48,2,512]{3,2,1,0:T(2,128)(2,1)}, bf16[1,48,2,512]{3,2,1,0:T(2,128)(2,1)S(1)}, u32[]{:S(2)}, u32[]{:S(2)}) collective-permute-start(bf16[1,48,2,512]{3,2,1,0:T(2,128)(2,1)} %get-tuple-element.41), channel_id=1, source_target_pairs={{0,2},{1,12},{2,0},{3,14},{4,6},{5,8},{6,4},{7,10},{8,5},{9,11},{1... | collective-permute-start | bytes 294920 | tf_op jit(solution)/shard_map/ppermute | solution.py:278
  28.8 10.3 %collective-permute-start.14 = (bf16[1,48,2,512]{3,2,1,0:T(2,128)(2,1)}, bf16[1,48,2,512]{3,2,1,0:T(2,128)(2,1)S(1)}, u32[]{:S(2)}, u32[]{:S(2)}) collective-permute-start(bf16[1,48,2,512]{3,2,1,0:T(2,128)(2,1)} %get-tuple-element.42), channel_id=1, source_target_pairs={{0,14},{1,2},{2,1},{3,13},{4,10},{5,6},{6,5},{7,9},{8,11},{9,7},{1... | collective-permute-start | bytes 294920 | tf_op jit(solution)/shard_map/ppermute | solution.py:278
  29.5 12.1 %collective-permute-start.15 = (bf16[1,48,2,512]{3,2,1,0:T(2,128)(2,1)}, bf16[1,48,2,512]{3,2,1,0:T(2,128)(2,1)S(1)}, u32[]{:S(2)}, u32[]{:S(2)}) collective-permute-start(bf16[1,48,2,512]{3,2,1,0:T(2,128)(2,1)} %get-tuple-element.43), channel_id=1, source_target_pairs={{0,3},{1,15},{2,12},{3,0},{4,7},{5,11},{6,8},{7,4},{8,6},{9,10},{1... | collective-permute-start | bytes 294920 | tf_op jit(solution)/shard_map/ppermute | solution.py:278
  32.6 11.0 %collective-permute-start.16 = (bf16[1,48,2,512]{3,2,1,0:T(2,128)(2,1)}, bf16[1,48,2,512]{3,2,1,0:T(2,128)(2,1)S(1)}, u32[]{:S(2)}, u32[]{:S(2)}) collective-permute-start(bf16[1,48,2,512]{3,2,1,0:T(2,128)(2,1)} %get-tuple-element.44), channel_id=1, source_target_pairs={{0,15},{1,14},{2,13},{3,12},{4,11},{5,10},{6,9},{7,8},{8,7},{9,6},... | collective-permute-start | bytes 294920 | tf_op jit(solution)/shard_map/ppermute | solution.py:278
  34.8 0.9 %copy-start = (bf16[1,48,2,512]{3,2,1,0:T(2,128)(2,1)S(1)}, bf16[1,48,2,512]{3,2,1,0:T(2,128)(2,1)}, u32[]{:S(2)}) copy-start(bf16[1,48,2,512]{3,2,1,0:T(2,128)(2,1)} %get-tuple-element.27.own) | copy-start | bytes 294916
  35.7 0.8 %copy-start.1 = (bf16[2,128,128]{2,1,0:T(8,128)(2,1)S(1)}, bf16[2,128,128]{2,1,0:T(8,128)(2,1)}, u32[]{:S(2)}) copy-start(bf16[2,128,128]{2,1,0:T(8,128)(2,1)} %get-tuple-element.25.sink) | copy-start | bytes 196612
  36.5 0.8 %copy-start.2 = (bf16[2,128,128]{2,1,0:T(8,128)(2,1)S(1)}, bf16[2,128,128]{2,1,0:T(8,128)(2,1)}, u32[]{:S(2)}) copy-start(bf16[2,128,128]{2,1,0:T(8,128)(2,1)} %get-tuple-element.26.source) | copy-start | bytes 196612
where the time goes:
time: 48.7 us; the launch traced here: 48.4 us
  starting transfers between devices  26 us (53%)
  Pallas kernels  9.61 us (20%)
  waiting for transfers between devices  8.37 us (17%)
  local copies, waits for them, and re-layouts  3.65 us (7%)
  between operations  0.72 us (1%)
    ppermute x15, starting transfers between devices, exchange(): received.append(lax.ppermute(block, 'ta', step_pairs(step, devices)))  23.1 us
    ppermute x15, waiting for transfers between devices, exchange(): received.append(lax.ppermute(block, 'ta', step_pairs(step, devices)))  8.37 us
    pallas_call x1, Pallas kernels, pair_loop(): pl.pallas_call(functools.partial(pair_kernel, batches_of), out_shape=jax....  4.75 us
    pallas_call x1, Pallas kernels, cut_blocks(): pl.pallas_call(functools.partial(cut_kernel, steps), out_shape=[jax.Shape...  3.14 us
    ppermute x2, starting transfers between devices, exchange(): tallies.append(lax.ppermute(counts, 'ta', step_pairs(step, devices)))  2.93 us
    unnamed x6, local copies, waits for them, and re-layouts  2.57 us
    pallas_call x1, Pallas kernels, operators(): pl.pallas_call(functools.partial(operators_kernel, len(counts)), out_shap...  1.72 us
    dynamic_slice x1, local copies, waits for them, and re-layouts, exchange(): lax.dynamic_slice_in_dim(outgoing, rank ^ step_mask(step, rank), 1)  1.08 us
  transfers between devices with their start and end apart: 17, of which 5 were waited for; matrix products, arithmetic and copies ran while one was open for 2% of the time, Pallas kernels for 10%

commit v1 on v0

--- a/solution.py
+++ b/solution.py
@@ -117,9 +117,9 @@
             pltpu.SemaphoreType.DMA((max(len(steps), 1),)),
         ],
         cost_estimate=pl.CostEstimate(flops=0, bytes_accessed=3 * 10**6, transcendentals=0),
-        compiler_params=pltpu.CompilerParams(vmem_limit_bytes=60 * 2**20),
+        compiler_params=pltpu.CompilerParams(vmem_limit_bytes=8 * 2**20),
         name="cut_blocks",
-    )(counts, sink_operator, columns, sink_elemental, source_elemental)
+    )(counts, sink_operator, *[pltpu.with_memory_space_constraint(x, pltpu.HBM) for x in (columns, sink_elemental, source_elemental)])
     return blocks, sink, source
 
 
@@ -130,20 +130,23 @@
     def place(array, index, batch):
         count, start = table[0, batch], table[1, batch]
 
+        def move(first, columns):
+            value = array[index, pl.ds(first, columns)]
+            for spin in range(spins):
+                packed[spin, pl.ds(start + first, columns)] = value[:, :, n * spin : n * (spin + 1)]
+
+        def several(group, carry):
+            move(jnp.minimum(group * unroll, count - unroll), unroll)
+            return carry
+
         def one(column, carry):
-            value = array[index, column]
-            for spin in range(spins):
-                packed[spin, start + column] = value[:, n * spin : n * (spin + 1)]
+            move(column, 1)
             return carry
 
-        def several(group, carry):
-            for column in range(unroll):
-                one(group * unroll + column, carry)
-            return carry
-
-        whole = count // unroll
-        lax.fori_loop(0, whole, several, 0)
-        lax.fori_loop(whole * unroll, count, one, 0)
+        small = count < unroll
+        if array.shape[1] >= unroll:
+            lax.fori_loop(0, jnp.where(small, 0, (count + unroll - 1) // unroll), several, 0)
+        lax.fori_loop(0, jnp.where(small, count, 0), one, 0)
 
     for array, batch in zip(arrays, sources):
         if batch is None:
@@ -230,10 +233,7 @@
 
 
 def exchange_steps(devices):
-    far, near, low = list(range(devices // 2, devices)), [], devices // 4
-    while low > 1:
-        near += range(low, 2 * low)
-        low //= 2
+    far, near = range(devices // 2, devices), range(2, devices // 2)
     steps = [(far[0], far[0], 1)]
     for number, (a, b) in enumerate(zip(far[1:-1], near)):
         classes = [c for c in range(1, devices) if parity(c & a) == 0 and parity(c & b) == 0]

time: 48.7 us -> 48.1 us (0.988)
  the two profiles are of different devices: /device:TPU:9 before, /device:TPU:0 now
where the time goes in v1:
time: 48.1 us; the launch traced here: 47.8 us
  starting transfers between devices  24.8 us (52%)
  waiting for transfers between devices  12.5 us (26%)
  Pallas kernels  8.01 us (17%)
  local copies, waits for them, and re-layouts  1.75 us (4%)
  between operations  0.72 us (1%)
    ppermute x15, starting transfers between devices, exchange(): received.append(lax.ppermute(block, 'ta', step_pairs(step, devices)))  19.3 us
    ppermute x15, waiting for transfers between devices, exchange(): received.append(lax.ppermute(block, 'ta', step_pairs(step, devices)))  12.5 us
    ppermute x2, starting transfers between devices, exchange(): tallies.append(lax.ppermute(counts, 'ta', step_pairs(step, devices)))  5.56 us
    pallas_call x1, Pallas kernels, pair_loop(): pl.pallas_call(functools.partial(pair_kernel, batches_of), out_shape=jax....  4.7 us
    pallas_call x1, Pallas kernels, cut_blocks(): pl.pallas_call(functools.partial(cut_kernel, steps), out_shape=[jax.Shape...  1.7 us
    pallas_call x1, Pallas kernels, operators(): pl.pallas_call(functools.partial(operators_kernel, len(counts)), out_shap...  1.6 us
    dynamic_slice x1, local copies, waits for them, and re-layouts, exchange(): lax.dynamic_slice_in_dim(outgoing, rank ^ step_mask(step, rank), 1)  1.08 us
  transfers between devices with their start and end apart: 17, of which 5 were waited for; matrix products, arithmetic and copies ran while one was open for 2% of the time, Pallas kernels for 7%

profile of v1, /device:TPU:0, one launch (start us, length us, event | category | flops | bytes accessed | tf_op | source)
XLA Modules:
  0.0 47.8 jit_solution(10372268380649154839)
XLA Ops:
  0.0 3.5 %collective-permute-start.1 = (s32[1]{0:T(128)}, s32[1]{0:T(128)}, u32[]{:S(2)}, u32[]{:S(2)}) collective-permute-start(s32[1]{0:T(128)} %param.6), channel_id=1, source_target_pairs={{0,9},{1,3},{2,11},{3,1},{4,13},{5,7},{6,15},{7,5},{8,10},{9,0},{1... | collective-permute-start | bytes 20 | tf_op jit(solution)/shard_map/ppermute | solution.py:275
  3.5 2.1 %collective-permute-start = (s32[1]{0:T(128)}, s32[1]{0:T(128)}, u32[]{:S(2)}, u32[]{:S(2)}) collective-permute-start(s32[1]{0:T(128)} %param.6), channel_id=1, source_target_pairs={{0,8},{1,9},{2,10},{3,11},{4,12},{5,13},{6,14},{7,15},{8,0},{9,1},... | collective-permute-start | bytes 20 | tf_op jit(solution)/shard_map/ppermute | solution.py:275
  5.6 1.1 %dynamic-slice_bitcast_fusion = (bf16[1,48,2,512]{3,2,1,0:T(2,128)(2,1)S(1)}, bf16[1,48,2,512]{3,2,1,0:T(2,128)(2,1)S(1)}) fusion(bf16[1,16,48,2,512]{4,3,2,1,0:T(2,128)(2,1)} %param.5, s32[]{:T(128)S(6)} %select_n.12, s32[]{:T(128)S(6)} %select_n.10), kind=kLoop, calls=%fused_computation | loop fusion | bytes 393224 | tf_op jit(solution)/shard_map/dynamic_slice | solution.py:271
  6.6 0.1 collective-permute-start.3
  6.7 2.4 %collective-permute-start.2 = (bf16[1,48,2,512]{3,2,1,0:T(2,128)(2,1)S(1)}, bf16[1,48,2,512]{3,2,1,0:T(2,128)(2,1)S(1)}, u32[]{:S(2)}, u32[]{:S(2)}) collective-permute-start(bf16[1,48,2,512]{3,2,1,0:T(2,128)(2,1)S(1)} %get-tuple-element.46), channel_id=1, source_target_pairs={{0,8},{1,9},{2,10},{3,11},{4,12},{5,13},{6,14},{7,15},{8,0},{9,1},... | collective-permute-start | bytes 294920 | tf_op jit(solution)/shard_map/ppermute | solution.py:278
  9.7 0.0 copy-start
  9.7 0.7 %copy-done = s32[2,16]{1,0:T(2,128)S(1)} copy-done((s32[2,16]{1,0:T(2,128)S(1)}, s32[2,16]{1,0:T(2,128)}, u32[]{:S(2)}) %copy-start) | copy-done | bytes 152
  10.4 1.7 %cut_blocks.1 = (bf16[1,48,2,512]{3,2,1,0:T(2,128)(2,1)S(1)}, bf16[1,48,2,512]{3,2,1,0:T(2,128)(2,1)S(1)}, bf16[1,48,2,512]{3,2,1,0:T(2,128)(2,1)S(1)}, bf16[1,4...) custom-call(s32[1]{0:T(128)S(6)} %copy.6.count_hbm, ...), custom_call_target="tpu_custom_call" | custom-call | bytes 3000000 | tf_op jit(solution)/shard_map/cut_blocks/pallas_call | solution.py:106
  12.1 0.6 %collective-permute-start.4 = (bf16[1,48,2,512]{3,2,1,0:T(2,128)(2,1)S(1)}, bf16[1,48,2,512]{3,2,1,0:T(2,128)(2,1)S(1)}, u32[]{:S(2)}, u32[]{:S(2)}) collective-permute-start(bf16[1,48,2,512]{3,2,1,0:T(2,128)(2,1)S(1)} %get-tuple-element.32), channel_id=1, source_target_pairs={{0,2},{1,8},{2,0},{3,10},{4,6},{5,12},{6,4},{7,14},{8,1},{9,11},{1... | collective-permute-start | bytes 294920 | tf_op jit(solution)/shard_map/ppermute | solution.py:278
  12.7 0.0 collective-permute-done.1.refs_1_
  12.7 2.4 %collective-permute-start.5 = (bf16[1,48,2,512]{3,2,1,0:T(2,128)(2,1)S(1)}, bf16[1,48,2,512]{3,2,1,0:T(2,128)(2,1)S(1)}, u32[]{:S(2)}, u32[]{:S(2)}) collective-permute-start(bf16[1,48,2,512]{3,2,1,0:T(2,128)(2,1)S(1)} %get-tuple-element.33), channel_id=1, source_target_pairs={{0,10},{1,2},{2,1},{3,9},{4,14},{5,6},{6,5},{7,13},{8,11},{9,3},{1... | collective-permute-start | bytes 294920 | tf_op jit(solution)/shard_map/ppermute | solution.py:278
  15.1 0.0 collective-permute-done.refs_0_
  15.1 0.0 collective-permute-start.6
  15.1 0.1 collective-permute-done.3.refs_5_
  15.2 2.3 %collective-permute-start.7 = (bf16[1,48,2,512]{3,2,1,0:T(2,128)(2,1)S(1)}, bf16[1,48,2,512]{3,2,1,0:T(2,128)(2,1)S(1)}, u32[]{:S(2)}, u32[]{:S(2)}) collective-permute-start(bf16[1,48,2,512]{3,2,1,0:T(2,128)(2,1)S(1)} %get-tuple-element.35), channel_id=1, source_target_pairs={{0,11},{1,5},{2,9},{3,7},{4,15},{5,1},{6,13},{7,3},{8,12},{9,2},{1... | collective-permute-start | bytes 294920 | tf_op jit(solution)/shard_map/ppermute | solution.py:278
  17.5 0.0 collective-permute-done.2.refs_4_
  17.5 1.6 %collective-permute-start.8 = (bf16[1,48,2,512]{3,2,1,0:T(2,128)(2,1)S(1)}, bf16[1,48,2,512]{3,2,1,0:T(2,128)(2,1)S(1)}, u32[]{:S(2)}, u32[]{:S(2)}) collective-permute-start(bf16[1,48,2,512]{3,2,1,0:T(2,128)(2,1)S(1)} %get-tuple-element.36), channel_id=1, source_target_pairs={{0,4},{1,10},{2,6},{3,8},{4,0},{5,14},{6,2},{7,12},{8,3},{9,13},{1... | collective-permute-start | bytes 294920 | tf_op jit(solution)/shard_map/ppermute | solution.py:278
  19.1 0.0 collective-permute-done.4.refs_6_
  19.1 1.4 %collective-permute-start.9 = (bf16[1,48,2,512]{3,2,1,0:T(2,128)(2,1)S(1)}, bf16[1,48,2,512]{3,2,1,0:T(2,128)(2,1)S(1)}, u32[]{:S(2)}, u32[]{:S(2)}) collective-permute-start(bf16[1,48,2,512]{3,2,1,0:T(2,128)(2,1)S(1)} %get-tuple-element.37), channel_id=1, source_target_pairs={{0,12},{1,4},{2,14},{3,6},{4,1},{5,9},{6,3},{7,11},{8,13},{9,5},{1... | collective-permute-start | bytes 294920 | tf_op jit(solution)/shard_map/ppermute | solution.py:278
  20.5 5.9 %collective-permute-done.5.refs_7_ = bf16[1,48,2,512]{3,2,1,0:T(2,128)(2,1)S(1)} collective-permute-done((bf16[1,48,2,512]{3,2,1,0:T(2,128)(2,1)S(1)}, bf16[1,48,2,512]{3,2,1,0:T(2,128)(2,1)S(1)}, u32[]{:S(2)}, u32[]{:S(2)}) %collective-permute-start.5) | collective-permute-done | bytes 98336 | tf_op jit(solution)/shard_map/ppermute | solution.py:278
  26.4 0.0 collective-permute-start.10
  26.4 0.0 collective-permute-done.6.refs_8_
  26.4 0.2 collective-permute-start.11
  26.6 1.7 %collective-permute-done.7.refs_9_ = bf16[1,48,2,512]{3,2,1,0:T(2,128)(2,1)S(1)} collective-permute-done((bf16[1,48,2,512]{3,2,1,0:T(2,128)(2,1)S(1)}, bf16[1,48,2,512]{3,2,1,0:T(2,128)(2,1)S(1)}, u32[]{:S(2)}, u32[]{:S(2)}) %collective-permute-start.7) | collective-permute-done | bytes 98336 | tf_op jit(solution)/shard_map/ppermute | solution.py:278
  28.4 1.3 %collective-permute-start.12 = (bf16[1,48,2,512]{3,2,1,0:T(2,128)(2,1)S(1)}, bf16[1,48,2,512]{3,2,1,0:T(2,128)(2,1)S(1)}, u32[]{:S(2)}, u32[]{:S(2)}) collective-permute-start(bf16[1,48,2,512]{3,2,1,0:T(2,128)(2,1)S(1)} %get-tuple-element.40), channel_id=1, source_target_pairs={{0,13},{1,7},{2,15},{3,5},{4,9},{5,3},{6,11},{7,1},{8,14},{9,4},{1... | collective-permute-start | bytes 294920 | tf_op jit(solution)/shard_map/ppermute | solution.py:278
  29.7 0.0 collective-permute-done.8.refs_10_
  29.7 0.0 collective-permute-start.13
  29.7 0.0 collective-permute-done.9.refs_11_
  29.7 4.8 %collective-permute-start.14 = (bf16[1,48,2,512]{3,2,1,0:T(2,128)(2,1)S(1)}, bf16[1,48,2,512]{3,2,1,0:T(2,128)(2,1)S(1)}, u32[]{:S(2)}, u32[]{:S(2)}) collective-permute-start(bf16[1,48,2,512]{3,2,1,0:T(2,128)(2,1)S(1)} %get-tuple-element.42), channel_id=1, source_target_pairs={{0,14},{1,6},{2,12},{3,4},{4,3},{5,11},{6,1},{7,9},{8,15},{9,7},{1... | collective-permute-start | bytes 294920 | tf_op jit(solution)/shard_map/ppermute | solution.py:278
  34.5 0.0 collective-permute-done.10.refs_12_
  34.5 0.0 collective-permute-start.15
  34.5 0.0 collective-permute-done.11.refs_13_
  34.5 2.3 %collective-permute-start.16 = (bf16[1,48,2,512]{3,2,1,0:T(2,128)(2,1)S(1)}, bf16[1,48,2,512]{3,2,1,0:T(2,128)(2,1)S(1)}, u32[]{:S(2)}, u32[]{:S(2)}) collective-permute-start(bf16[1,48,2,512]{3,2,1,0:T(2,128)(2,1)S(1)} %get-tuple-element.44), channel_id=1, source_target_pairs={{0,15},{1,14},{2,13},{3,12},{4,11},{5,10},{6,9},{7,8},{8,7},{9,6},... | collective-permute-start | bytes 294920 | tf_op jit(solution)/shard_map/ppermute | solution.py:278
  36.8 1.6 %operators.1 = (bf16[512,256]{1,0:T(8,128)(2,1)S(1)}, bf16[256,256]{1,0:T(8,128)(2,1)S(1)}, bf16[1,48,2,512]{3,2,1,0:T(2,128)(2,1)S(1)}, f32[2,8,128]{2,1,0:T(8,128)S(1)}) custom-call(bf16[2,128,128]{2,1,0:T(8,128)(2,1)S(1)} %get-tuple-element.25.sink, bf16[2,128,128]{2,1,0:T(8,128)(2,1)S(1)} %get-tuple-element.26.source, ...), custom_call_target="tpu_custom_call" | custom-call | flops 100000000 | bytes 1000000 | tf_op jit(solution)/shard_map/operators/pallas_call | solution.py:54
  38.4 0.0 collective-permute-done.12.refs_14_
  38.4 0.0 collective-permute-done.13.refs_15_
  38.4 1.4 %collective-permute-done.14.refs_16_ = bf16[1,48,2,512]{3,2,1,0:T(2,128)(2,1)S(1)} collective-permute-done((bf16[1,48,2,512]{3,2,1,0:T(2,128)(2,1)S(1)}, bf16[1,48,2,512]{3,2,1,0:T(2,128)(2,1)S(1)}, u32[]{:S(2)}, u32[]{:S(2)}) %collective-permute-start.14) | collective-permute-done | bytes 98336 | tf_op jit(solution)/shard_map/ppermute | solution.py:278
  39.8 3.4 %collective-permute-done.15.refs_17_ = bf16[1,48,2,512]{3,2,1,0:T(2,128)(2,1)S(1)} collective-permute-done((bf16[1,48,2,512]{3,2,1,0:T(2,128)(2,1)S(1)}, bf16[1,48,2,512]{3,2,1,0:T(2,128)(2,1)S(1)}, u32[]{:S(2)}, u32[]{:S(2)}) %collective-permute-start.15) | collective-permute-done | bytes 98336 | tf_op jit(solution)/shard_map/ppermute | solution.py:278
  43.1 0.0 collective-permute-done.16.refs_18_
  43.1 4.7 %pair_loop.1 = bf16[2,512,512]{2,1,0:T(8,128)(2,1)} custom-call(bf16[512,256]{1,0:T(8,128)(2,1)S(1)} %get-tuple-element.28.refs_0_, bf16[256,256]{1,0:T(8,128)(2,1)S(1)} %get-tuple-element.29.refs_1_, f32[2,8,128]{2,1,0:T(8,128)S(1)} %get-tuple-element.30.refs_2_, bf16[1,48,2,512]{3,2,1,0:T(2,128)(2,1)S(1)} %get-tuple-element.31.refs_3_, ...), custom_call_target="tpu_custom_call" | custom-call | flops 2000000000 | bytes 3000000 | tf_op jit(solution)/shard_map/pair_loop/pallas_call | solution.py:213
Async XLA Ops:
  0.0 12.7 %collective-permute-start.1 = (s32[1]{0:T(128)}, s32[1]{0:T(128)}, u32[]{:S(2)}, u32[]{:S(2)}) collective-permute-start(s32[1]{0:T(128)} %param.6), channel_id=1, source_target_pairs={{0,9},{1,3},{2,11},{3,1},{4,13},{5,7},{6,15},{7,5},{8,10},{9,0},{1... | collective-permute-start | bytes 20 | tf_op jit(solution)/shard_map/ppermute | solution.py:275
  3.5 11.6 %collective-permute-start = (s32[1]{0:T(128)}, s32[1]{0:T(128)}, u32[]{:S(2)}, u32[]{:S(2)}) collective-permute-start(s32[1]{0:T(128)} %param.6), channel_id=1, source_target_pairs={{0,8},{1,9},{2,10},{3,11},{4,12},{5,13},{6,14},{7,15},{8,0},{9,1},... | collective-permute-start | bytes 20 | tf_op jit(solution)/shard_map/ppermute | solution.py:275
  6.6 8.6 %collective-permute-start.3 = (bf16[1,48,2,512]{3,2,1,0:T(2,128)(2,1)S(1)}, bf16[1,48,2,512]{3,2,1,0:T(2,128)(2,1)S(1)}, u32[]{:S(2)}, u32[]{:S(2)}) collective-permute-start(bf16[1,48,2,512]{3,2,1,0:T(2,128)(2,1)S(1)} %get-tuple-element.45), channel_id=1, source_target_pairs={{0,9},{1,3},{2,11},{3,1},{4,13},{5,7},{6,15},{7,5},{8,10},{9,0},{1... | collective-permute-start | bytes 294920 | tf_op jit(solution)/shard_map/ppermute | solution.py:278
  6.7 10.8 %collective-permute-start.2 = (bf16[1,48,2,512]{3,2,1,0:T(2,128)(2,1)S(1)}, bf16[1,48,2,512]{3,2,1,0:T(2,128)(2,1)S(1)}, u32[]{:S(2)}, u32[]{:S(2)}) collective-permute-start(bf16[1,48,2,512]{3,2,1,0:T(2,128)(2,1)S(1)} %get-tuple-element.46), channel_id=1, source_target_pairs={{0,8},{1,9},{2,10},{3,11},{4,12},{5,13},{6,14},{7,15},{8,0},{9,1},... | collective-permute-start | bytes 294920 | tf_op jit(solution)/shard_map/ppermute | solution.py:278
  9.7 0.7 %copy-start = (s32[2,16]{1,0:T(2,128)S(1)}, s32[2,16]{1,0:T(2,128)}, u32[]{:S(2)}) copy-start(s32[2,16]{1,0:T(2,128)} %operator_hbm.1) | copy-start | bytes 388
  12.1 7.0 %collective-permute-start.4 = (bf16[1,48,2,512]{3,2,1,0:T(2,128)(2,1)S(1)}, bf16[1,48,2,512]{3,2,1,0:T(2,128)(2,1)S(1)}, u32[]{:S(2)}, u32[]{:S(2)}) collective-permute-start(bf16[1,48,2,512]{3,2,1,0:T(2,128)(2,1)S(1)} %get-tuple-element.32), channel_id=1, source_target_pairs={{0,2},{1,8},{2,0},{3,10},{4,6},{5,12},{6,4},{7,14},{8,1},{9,11},{1... | collective-permute-start | bytes 294920 | tf_op jit(solution)/shard_map/ppermute | solution.py:278
  12.7 13.7 %collective-permute-start.5 = (bf16[1,48,2,512]{3,2,1,0:T(2,128)(2,1)S(1)}, bf16[1,48,2,512]{3,2,1,0:T(2,128)(2,1)S(1)}, u32[]{:S(2)}, u32[]{:S(2)}) collective-permute-start(bf16[1,48,2,512]{3,2,1,0:T(2,128)(2,1)S(1)} %get-tuple-element.33), channel_id=1, source_target_pairs={{0,10},{1,2},{2,1},{3,9},{4,14},{5,6},{6,5},{7,13},{8,11},{9,3},{1... | collective-permute-start | bytes 294920 | tf_op jit(solution)/shard_map/ppermute | solution.py:278
  15.1 11.3 %collective-permute-start.6 = (bf16[1,48,2,512]{3,2,1,0:T(2,128)(2,1)S(1)}, bf16[1,48,2,512]{3,2,1,0:T(2,128)(2,1)S(1)}, u32[]{:S(2)}, u32[]{:S(2)}) collective-permute-start(bf16[1,48,2,512]{3,2,1,0:T(2,128)(2,1)S(1)} %get-tuple-element.34), channel_id=1, source_target_pairs={{0,3},{1,11},{2,8},{3,0},{4,7},{5,15},{6,12},{7,4},{8,2},{9,10},{1... | collective-permute-start | bytes 294920 | tf_op jit(solution)/shard_map/ppermute | solution.py:278
  15.2 13.2 %collective-permute-start.7 = (bf16[1,48,2,512]{3,2,1,0:T(2,128)(2,1)S(1)}, bf16[1,48,2,512]{3,2,1,0:T(2,128)(2,1)S(1)}, u32[]{:S(2)}, u32[]{:S(2)}) collective-permute-start(bf16[1,48,2,512]{3,2,1,0:T(2,128)(2,1)S(1)} %get-tuple-element.35), channel_id=1, source_target_pairs={{0,11},{1,5},{2,9},{3,7},{4,15},{5,1},{6,13},{7,3},{8,12},{9,2},{1... | collective-permute-start | bytes 294920 | tf_op jit(solution)/shard_map/ppermute | solution.py:278
  17.5 12.2 %collective-permute-start.8 = (bf16[1,48,2,512]{3,2,1,0:T(2,128)(2,1)S(1)}, bf16[1,48,2,512]{3,2,1,0:T(2,128)(2,1)S(1)}, u32[]{:S(2)}, u32[]{:S(2)}) collective-permute-start(bf16[1,48,2,512]{3,2,1,0:T(2,128)(2,1)S(1)} %get-tuple-element.36), channel_id=1, source_target_pairs={{0,4},{1,10},{2,6},{3,8},{4,0},{5,14},{6,2},{7,12},{8,3},{9,13},{1... | collective-permute-start | bytes 294920 | tf_op jit(solution)/shard_map/ppermute | solution.py:278
  19.1 10.6 %collective-permute-start.9 = (bf16[1,48,2,512]{3,2,1,0:T(2,128)(2,1)S(1)}, bf16[1,48,2,512]{3,2,1,0:T(2,128)(2,1)S(1)}, u32[]{:S(2)}, u32[]{:S(2)}) collective-permute-start(bf16[1,48,2,512]{3,2,1,0:T(2,128)(2,1)S(1)} %get-tuple-element.37), channel_id=1, source_target_pairs={{0,12},{1,4},{2,14},{3,6},{4,1},{5,9},{6,3},{7,11},{8,13},{9,5},{1... | collective-permute-start | bytes 294920 | tf_op jit(solution)/shard_map/ppermute | solution.py:278
  26.4 8.1 %collective-permute-start.10 = (bf16[1,48,2,512]{3,2,1,0:T(2,128)(2,1)S(1)}, bf16[1,48,2,512]{3,2,1,0:T(2,128)(2,1)S(1)}, u32[]{:S(2)}, u32[]{:S(2)}) collective-permute-start(bf16[1,48,2,512]{3,2,1,0:T(2,128)(2,1)S(1)} %get-tuple-element.38), channel_id=1, source_target_pairs={{0,5},{1,13},{2,7},{3,15},{4,8},{5,0},{6,10},{7,2},{8,4},{9,12},{1... | collective-permute-start | bytes 294920 | tf_op jit(solution)/shard_map/ppermute | solution.py:278
  26.4 8.1 %collective-permute-start.11 = (bf16[1,48,2,512]{3,2,1,0:T(2,128)(2,1)S(1)}, bf16[1,48,2,512]{3,2,1,0:T(2,128)(2,1)S(1)}, u32[]{:S(2)}, u32[]{:S(2)}) collective-permute-start(bf16[1,48,2,512]{3,2,1,0:T(2,128)(2,1)S(1)} %get-tuple-element.39), channel_id=1, source_target_pairs={{0,1},{1,0},{2,3},{3,2},{4,5},{5,4},{6,7},{7,6},{8,9},{9,8},{10,11... | collective-permute-start | bytes 294920 | tf_op jit(solution)/shard_map/ppermute | solution.py:278
  28.4 10.0 %collective-permute-start.12 = (bf16[1,48,2,512]{3,2,1,0:T(2,128)(2,1)S(1)}, bf16[1,48,2,512]{3,2,1,0:T(2,128)(2,1)S(1)}, u32[]{:S(2)}, u32[]{:S(2)}) collective-permute-start(bf16[1,48,2,512]{3,2,1,0:T(2,128)(2,1)S(1)} %get-tuple-element.40), channel_id=1, source_target_pairs={{0,13},{1,7},{2,15},{3,5},{4,9},{5,3},{6,11},{7,1},{8,14},{9,4},{1... | collective-permute-start | bytes 294920 | tf_op jit(solution)/shard_map/ppermute | solution.py:278
  29.7 8.7 %collective-permute-start.13 = (bf16[1,48,2,512]{3,2,1,0:T(2,128)(2,1)S(1)}, bf16[1,48,2,512]{3,2,1,0:T(2,128)(2,1)S(1)}, u32[]{:S(2)}, u32[]{:S(2)}) collective-permute-start(bf16[1,48,2,512]{3,2,1,0:T(2,128)(2,1)S(1)} %get-tuple-element.41), channel_id=1, source_target_pairs={{0,6},{1,12},{2,4},{3,14},{4,2},{5,8},{6,0},{7,10},{8,5},{9,15},{1... | collective-permute-start | bytes 294920 | tf_op jit(solution)/shard_map/ppermute | solution.py:278
  29.7 10.1 %collective-permute-start.14 = (bf16[1,48,2,512]{3,2,1,0:T(2,128)(2,1)S(1)}, bf16[1,48,2,512]{3,2,1,0:T(2,128)(2,1)S(1)}, u32[]{:S(2)}, u32[]{:S(2)}) collective-permute-start(bf16[1,48,2,512]{3,2,1,0:T(2,128)(2,1)S(1)} %get-tuple-element.42), channel_id=1, source_target_pairs={{0,14},{1,6},{2,12},{3,4},{4,3},{5,11},{6,1},{7,9},{8,15},{9,7},{1... | collective-permute-start | bytes 294920 | tf_op jit(solution)/shard_map/ppermute | solution.py:278
  34.5 8.6 %collective-permute-start.15 = (bf16[1,48,2,512]{3,2,1,0:T(2,128)(2,1)S(1)}, bf16[1,48,2,512]{3,2,1,0:T(2,128)(2,1)S(1)}, u32[]{:S(2)}, u32[]{:S(2)}) collective-permute-start(bf16[1,48,2,512]{3,2,1,0:T(2,128)(2,1)S(1)} %get-tuple-element.43), channel_id=1, source_target_pairs={{0,7},{1,15},{2,5},{3,13},{4,10},{5,2},{6,8},{7,0},{8,6},{9,14},{1... | collective-permute-start | bytes 294920 | tf_op jit(solution)/shard_map/ppermute | solution.py:278
  34.5 8.6 %collective-permute-start.16 = (bf16[1,48,2,512]{3,2,1,0:T(2,128)(2,1)S(1)}, bf16[1,48,2,512]{3,2,1,0:T(2,128)(2,1)S(1)}, u32[]{:S(2)}, u32[]{:S(2)}) collective-permute-start(bf16[1,48,2,512]{3,2,1,0:T(2,128)(2,1)S(1)} %get-tuple-element.44), channel_id=1, source_target_pairs={{0,15},{1,14},{2,13},{3,12},{4,11},{5,10},{6,9},{7,8},{8,7},{9,6},... | collective-permute-start | bytes 294920 | tf_op jit(solution)/shard_map/ppermute | solution.py:278

commit v2 on v1

--- a/solution.py
+++ b/solution.py
@@ -11,6 +11,7 @@
 SPINS = 4
 LARGEST_EXCHANGE = 32
 LEAD = 2
+LATE = 1
 
 f32 = jnp.float32
 bf16 = jnp.bfloat16
@@ -119,17 +120,15 @@
         cost_estimate=pl.CostEstimate(flops=0, bytes_accessed=3 * 10**6, transcendentals=0),
         compiler_params=pltpu.CompilerParams(vmem_limit_bytes=8 * 2**20),
         name="cut_blocks",
-    )(counts, sink_operator, *[pltpu.with_memory_space_constraint(x, pltpu.HBM) for x in (columns, sink_elemental, source_elemental)])
+    )(counts, *[pltpu.with_memory_space_constraint(x, pltpu.HBM) for x in (sink_operator, columns, sink_elemental, source_elemental)])
     return blocks, sink, source
 
 
-def place_blocks(table, sources, arrays, packed):
+def place_blocks(spans, arrays, packed):
     spins, _, _, n = packed.shape
     unroll = 8
 
-    def place(array, index, batch):
-        count, start = table[0, batch], table[1, batch]
-
+    def place(array, index, count, start):
         def move(first, columns):
             value = array[index, pl.ds(first, columns)]
             for spin in range(spins):
@@ -148,38 +147,70 @@
             lax.fori_loop(0, jnp.where(small, 0, (count + unroll - 1) // unroll), several, 0)
         lax.fori_loop(0, jnp.where(small, count, 0), one, 0)
 
-    for array, batch in zip(arrays, sources):
-        if batch is None:
-            lax.fori_loop(0, array.shape[0], lambda batch, carry, array=array: (place(array, batch, batch), carry)[1], 0)
+    for array, span in zip(arrays, spans):
+        if isinstance(span, tuple):
+            place(array, 0, *span)
         else:
-            place(array, 0, batch)
-
-
-def pair_kernel(batches_of, *refs):
-    f_ref, e_ref, told_ref, *arrays = refs[:-7]
-    out_hbm, packed, turned, right, result, table, sems = refs[-7:]
-    spins, order, _, n = packed.shape
+
+            def each(batch, carry, array=array, table=span):
+                place(array, batch, table[0, batch], table[1, batch])
+                return carry
+
+            lax.fori_loop(0, array.shape[0], each, 0)
+
+
+def early_kernel(batches_of, told_ref, *refs):
+    *arrays, packed, late_ref, table = refs
     if batches_of is None:
         *arrays, counts = arrays
         sources = [None]
         pltpu.sync_copy(counts, table.at[0])
     else:
-        sources = batches_of(lax.axis_index("ta"))
-        for number, (batch, array) in enumerate(zip(sources, arrays)):
-            _, capacity, _, _ = array.shape
+        sources, left = batches_of(lax.axis_index("ta")), packed.shape[1]
+        for number, batch in enumerate(sources[:-LATE]):
             if 1 <= number <= LEAD:
                 told = told_ref[number - 1]
             else:
-                last = array[0, capacity - 1, :, :128].astype(f32)
+                capacity = arrays[number].shape[1]
+                last = arrays[number][0, capacity - 1, :, :128].astype(f32)
                 told = jnp.where(last[:1] == jnp.inf, last[1:], float(capacity))
-            table[0, batch] = told[0, 0].astype(jnp.int32)
+            count = told[0, 0].astype(jnp.int32)
+            table[0, batch] = count
+            left = left - count
+        table[0, sources[-1]] = left
 
     def running(batch, start):
         table[1, batch] = start
         return start + table[0, batch]
 
     lax.fori_loop(0, table.shape[1], running, jnp.int32(0))
-    place_blocks(table, sources, arrays, packed)
+    for number, batch in enumerate(sources[len(arrays) :]):
+        for row in range(2):
+            late_ref[2 * number + row] = jnp.full(late_ref.shape[1:], table[row, batch], jnp.int32).astype(f32)
+    place_blocks([(table[0, batch], table[1, batch]) if batch is not None else table for batch in sources], arrays, packed)
+
+
+def pack_early(batches_of, arrays, told, batches, order):
+    return pl.pallas_call(
+        functools.partial(early_kernel, batches_of),
+        out_shape=(
+            jax.ShapeDtypeStruct((SPINS, order, 2, order // SPINS), bf16),
+            jax.ShapeDtypeStruct((2 * LATE, 8, 128), f32),
+        ),
+        in_specs=[VMEM] * (len(arrays) + 1),
+        out_specs=(VMEM, VMEM),
+        scratch_shapes=[pltpu.SMEM((2, batches), jnp.int32)],
+        cost_estimate=pl.CostEstimate(flops=10**8, bytes_accessed=10**6, transcendentals=0),
+        compiler_params=pltpu.CompilerParams(vmem_limit_bytes=8 * 2**20),
+        name="pack_early",
+    )(told, *arrays)
+
+
+def pair_kernel(f_ref, e_ref, late_ref, *refs):
+    *arrays, _, packed, out_hbm, turned, right, result, sems = refs
+    spins, order, _, n = packed.shape
+    scalar = lambda row: late_ref[row][0, 0].astype(jnp.int32)
+    place_blocks([(scalar(2 * number), scalar(2 * number + 1)) for number in range(len(arrays))], arrays, packed)
     rows = packed.reshape(spins, 2 * order, n)
     half, per_half = order // 2, spins // 2
     for spin in range(spins):
@@ -208,25 +239,24 @@
         copy.wait()
 
 
-def pair_loop(batches_of, arrays, f_matrix, e_matrix, told, batches, order):
-    n = order // SPINS
+def pair_loop(arrays, packed, f_matrix, e_matrix, late):
+    _, order, _, _ = packed.shape
     return pl.pallas_call(
-        functools.partial(pair_kernel, batches_of),
-        out_shape=jax.ShapeDtypeStruct((2, order, order), bf16),
-        in_specs=[VMEM] * (len(arrays) + 3),
-        out_specs=HBM,
+        pair_kernel,
+        out_shape=(jax.ShapeDtypeStruct(packed.shape, bf16), jax.ShapeDtypeStruct((2, order, order), bf16)),
+        in_specs=[VMEM] * (len(arrays) + 4),
+        out_specs=(VMEM, HBM),
         scratch_shapes=[
-            pltpu.VMEM((SPINS, order, 2, n), bf16),
             pltpu.VMEM((order, 2 * order), bf16),
             pltpu.VMEM((2, 2 * order, order), bf16),
             pltpu.VMEM((2, order, order), bf16),
-            pltpu.SMEM((2, batches), jnp.int32),
             pltpu.SemaphoreType.DMA((2,)),
         ],
+        input_output_aliases={3 + len(arrays): 0},
         cost_estimate=pl.CostEstimate(flops=2 * 10**9, bytes_accessed=3 * 10**6, transcendentals=0),
         compiler_params=pltpu.CompilerParams(vmem_limit_bytes=24 * 2**20),
         name="pair_loop",
-    )(f_matrix, e_matrix, told, *arrays)
+    )(f_matrix, e_matrix, late, *arrays, packed)[1]
 
 
 OWN = (0, 0, 1)
@@ -287,15 +317,18 @@
     rank = lax.axis_index("ta").astype(jnp.int32)
     outgoing = perambulator.reshape(devices, capacity, parts, order)
     cut = functools.partial(cut_blocks, batch_columns, sink_operator, outgoing, sink_elemental, source_elemental)
+    late = []
     if exchanged(devices):
         arrays, f_matrix, e_matrix, told, batches_of = exchange(outgoing, batch_columns, rank, cut)
+        arrays, late = arrays[:-LATE], arrays[-LATE:]
     else:
         _, sink, source = cut([])
         arrays = [lax.all_to_all(outgoing, "ta", split_axis=0, concat_axis=0, tiled=True)]
         arrays.append(lax.all_gather(batch_columns, "ta", axis=0, tiled=True))
         f_matrix, e_matrix, _, told = operators(sink, source, sink, [])
         batches_of = None
-    return pair_loop(batches_of, arrays, f_matrix, e_matrix, told, devices, order)[None]
+    packed, spans = pack_early(batches_of, arrays, told, devices, order)
+    return pair_loop(late, packed, f_matrix, e_matrix, spans)[None]
 
 
 def exchanged(devices):

time: 48.1 us -> 51.6 us (1.073)
  starting transfers between devices: 24.8 us -> 28.4 us
  local copies, waits for them, and re-layouts: 1.75 us -> 1.08 us
  Pallas kernels: 8.01 us -> 8.55 us
    ppermute x15, starting transfers between devices: 19.3 us -> 26.2 us  [exchange(): received.append(lax.ppermute(block, 'ta', step_pairs(step, devices)))]
    ppermute x2, waiting for transfers between devices: 0.01 us -> 6.84 us  [exchange(): tallies.append(lax.ppermute(counts, 'ta', step_pairs(step, devices)))]
    ppermute x15, waiting for transfers between devices: 12.5 us -> 5.8 us  [exchange(): received.append(lax.ppermute(block, 'ta', step_pairs(step, devices)))]
    ppermute x2, starting transfers between devices: 5.56 us -> 2.15 us  [exchange(): tallies.append(lax.ppermute(counts, 'ta', step_pairs(step, devices)))]
    unnamed x2 -> x0, local copies, waits for them, and re-layouts: 0.67 us -> none
    pallas_call x1 -> x2, Pallas kernels: 4.7 us -> 4.86 us  [the longest x1 3.23 us: pair_loop(): pl.pallas_call(pair_kernel, out_shape=(jax.ShapeDtypeStruct(packed.shape,...]
  transfers between devices with their start and end apart: 17 -> 17, of which waited for: 5 -> 5; matrix products, arithmetic and copies ran while one was open for 2% -> 0% of each run, Pallas kernels for 7% -> 10%
where the time goes in v2:
time: 51.6 us; the launch traced here: 51.4 us
  starting transfers between devices  28.4 us (55%)
  waiting for transfers between devices  12.6 us (24%)
  Pallas kernels  8.55 us (17%)
  local copies, waits for them, and re-layouts  1.08 us (2%)
  between operations  0.72 us (1%)
    ppermute x15, starting transfers between devices, exchange(): received.append(lax.ppermute(block, 'ta', step_pairs(step, devices)))  26.2 us
    ppermute x2, waiting for transfers between devices, exchange(): tallies.append(lax.ppermute(counts, 'ta', step_pairs(step, devices)))  6.84 us
    ppermute x15, waiting for transfers between devices, exchange(): received.append(lax.ppermute(block, 'ta', step_pairs(step, devices)))  5.8 us
    pallas_call x1, Pallas kernels, pair_loop(): pl.pallas_call(pair_kernel, out_shape=(jax.ShapeDtypeStruct(packed.shape,...  3.23 us
    ppermute x2, starting transfers between devices, exchange(): tallies.append(lax.ppermute(counts, 'ta', step_pairs(step, devices)))  2.15 us
    pallas_call x1, Pallas kernels, cut_blocks(): pl.pallas_call(functools.partial(cut_kernel, steps), out_shape=[jax.Shape...  2.01 us
    pallas_call x1, Pallas kernels, operators(): pl.pallas_call(functools.partial(operators_kernel, len(counts)), out_shap...  1.67 us
    pallas_call x1, Pallas kernels, pack_early(): pl.pallas_call(functools.partial(early_kernel, batches_of), out_shape=(ja...  1.63 us
  transfers between devices with their start and end apart: 17, of which 5 were waited for; matrix products, arithmetic and copies ran while one was open for 0% of the time, Pallas kernels for 10%

profile of v2, /device:TPU:0, one launch (start us, length us, event | category | flops | bytes accessed | tf_op | source)
XLA Modules:
  0.0 51.4 jit_solution(209362686766005396)
XLA Ops:
  0.0 1.1 %dynamic-slice_bitcast_fusion = (bf16[1,48,2,512]{3,2,1,0:T(2,128)(2,1)S(1)}, bf16[1,48,2,512]{3,2,1,0:T(2,128)(2,1)S(1)}) fusion(bf16[1,16,48,2,512]{4,3,2,1,0:T(2,128)(2,1)} %param.5, s32[]{:T(128)S(6)} %select_n.12, s32[]{:T(128)S(6)} %select_n.10), kind=kLoop, calls=%fused_computation | loop fusion | bytes 393224 | tf_op jit(solution)/shard_map/dynamic_slice | solution.py:301
  1.1 3.6 %collective-permute-start.3 = (bf16[1,48,2,512]{3,2,1,0:T(2,128)(2,1)S(1)}, bf16[1,48,2,512]{3,2,1,0:T(2,128)(2,1)S(1)}, u32[]{:S(2)}, u32[]{:S(2)}) collective-permute-start(bf16[1,48,2,512]{3,2,1,0:T(2,128)(2,1)S(1)} %get-tuple-element.51), channel_id=1, source_target_pairs={{0,9},{1,3},{2,11},{3,1},{4,13},{5,7},{6,15},{7,5},{8,10},{9,0},{1... | collective-permute-start | bytes 294920 | tf_op jit(solution)/shard_map/ppermute | solution.py:308
  4.7 2.1 %collective-permute-start.2 = (bf16[1,48,2,512]{3,2,1,0:T(2,128)(2,1)S(1)}, bf16[1,48,2,512]{3,2,1,0:T(2,128)(2,1)S(1)}, u32[]{:S(2)}, u32[]{:S(2)}) collective-permute-start(bf16[1,48,2,512]{3,2,1,0:T(2,128)(2,1)S(1)} %get-tuple-element.52), channel_id=1, source_target_pairs={{0,8},{1,9},{2,10},{3,11},{4,12},{5,13},{6,14},{7,15},{8,0},{9,1},... | collective-permute-start | bytes 294920 | tf_op jit(solution)/shard_map/ppermute | solution.py:308
  7.4 2.0 %cut_blocks.1 = (bf16[1,48,2,512]{3,2,1,0:T(2,128)(2,1)S(1)}, bf16[1,48,2,512]{3,2,1,0:T(2,128)(2,1)S(1)}, bf16[1,48,2,512]{3,2,1,0:T(2,128)(2,1)S(1)}, bf16[1,4...) custom-call(s32[1]{0:T(128)S(6)} %copy.8.count_hbm, ...), custom_call_target="tpu_custom_call" | custom-call | bytes 3000000 | tf_op jit(solution)/shard_map/cut_blocks/pallas_call | solution.py:107
  9.4 0.6 %collective-permute-start.4 = (bf16[1,48,2,512]{3,2,1,0:T(2,128)(2,1)S(1)}, bf16[1,48,2,512]{3,2,1,0:T(2,128)(2,1)S(1)}, u32[]{:S(2)}, u32[]{:S(2)}) collective-permute-start(bf16[1,48,2,512]{3,2,1,0:T(2,128)(2,1)S(1)} %get-tuple-element.35), channel_id=1, source_target_pairs={{0,2},{1,8},{2,0},{3,10},{4,6},{5,12},{6,4},{7,14},{8,1},{9,11},{1... | collective-permute-start | bytes 294920 | tf_op jit(solution)/shard_map/ppermute | solution.py:308
  10.0 1.6 %collective-permute-start.5 = (bf16[1,48,2,512]{3,2,1,0:T(2,128)(2,1)S(1)}, bf16[1,48,2,512]{3,2,1,0:T(2,128)(2,1)S(1)}, u32[]{:S(2)}, u32[]{:S(2)}) collective-permute-start(bf16[1,48,2,512]{3,2,1,0:T(2,128)(2,1)S(1)} %get-tuple-element.36), channel_id=1, source_target_pairs={{0,10},{1,2},{2,1},{3,9},{4,14},{5,6},{6,5},{7,13},{8,11},{9,3},{1... | collective-permute-start | bytes 294920 | tf_op jit(solution)/shard_map/ppermute | solution.py:308
  11.6 2.0 %collective-permute-start.1 = (s32[1]{0:T(128)}, s32[1]{0:T(128)}, u32[]{:S(2)}, u32[]{:S(2)}) collective-permute-start(s32[1]{0:T(128)} %param.6), channel_id=1, source_target_pairs={{0,9},{1,3},{2,11},{3,1},{4,13},{5,7},{6,15},{7,5},{8,10},{9,0},{1... | collective-permute-start | bytes 20 | tf_op jit(solution)/shard_map/ppermute | solution.py:305
  13.6 2.3 %collective-permute-done.1.refs_1_ = s32[1]{0:T(128)} collective-permute-done((s32[1]{0:T(128)}, s32[1]{0:T(128)}, u32[]{:S(2)}, u32[]{:S(2)}) %collective-permute-start.1) | collective-permute-done | bytes 36 | tf_op jit(solution)/shard_map/ppermute | solution.py:305
  15.9 0.1 collective-permute-start
  16.0 4.6 %collective-permute-done.refs_0_ = s32[1]{0:T(128)} collective-permute-done((s32[1]{0:T(128)}, s32[1]{0:T(128)}, u32[]{:S(2)}, u32[]{:S(2)}) %collective-permute-start) | collective-permute-done | bytes 36 | tf_op jit(solution)/shard_map/ppermute | solution.py:305
  20.6 0.0 collective-permute-start.6
  20.6 0.0 collective-permute-done.3.refs_2_
  20.6 1.5 %collective-permute-start.7 = (bf16[1,48,2,512]{3,2,1,0:T(2,128)(2,1)S(1)}, bf16[1,48,2,512]{3,2,1,0:T(2,128)(2,1)S(1)}, u32[]{:S(2)}, u32[]{:S(2)}) collective-permute-start(bf16[1,48,2,512]{3,2,1,0:T(2,128)(2,1)S(1)} %get-tuple-element.38), channel_id=1, source_target_pairs={{0,11},{1,5},{2,9},{3,7},{4,15},{5,1},{6,13},{7,3},{8,12},{9,2},{1... | collective-permute-start | bytes 294920 | tf_op jit(solution)/shard_map/ppermute | solution.py:308
  22.0 0.0 collective-permute-done.2.refs_1_
  22.0 2.4 %collective-permute-start.8 = (bf16[1,48,2,512]{3,2,1,0:T(2,128)(2,1)S(1)}, bf16[1,48,2,512]{3,2,1,0:T(2,128)(2,1)S(1)}, u32[]{:S(2)}, u32[]{:S(2)}) collective-permute-start(bf16[1,48,2,512]{3,2,1,0:T(2,128)(2,1)S(1)} %get-tuple-element.39), channel_id=1, source_target_pairs={{0,4},{1,10},{2,6},{3,8},{4,0},{5,14},{6,2},{7,12},{8,3},{9,13},{1... | collective-permute-start | bytes 294920 | tf_op jit(solution)/shard_map/ppermute | solution.py:308
  24.5 0.0 collective-permute-done.4.refs_3_
  24.5 1.4 %collective-permute-start.9 = (bf16[1,48,2,512]{3,2,1,0:T(2,128)(2,1)S(1)}, bf16[1,48,2,512]{3,2,1,0:T(2,128)(2,1)S(1)}, u32[]{:S(2)}, u32[]{:S(2)}) collective-permute-start(bf16[1,48,2,512]{3,2,1,0:T(2,128)(2,1)S(1)} %get-tuple-element.40), channel_id=1, source_target_pairs={{0,12},{1,4},{2,14},{3,6},{4,1},{5,9},{6,3},{7,11},{8,13},{9,5},{1... | collective-permute-start | bytes 294920 | tf_op jit(solution)/shard_map/ppermute | solution.py:308
  25.9 0.0 collective-permute-done.5.refs_4_
  25.9 0.0 collective-permute-start.10
  25.9 0.0 collective-permute-done.6.refs_5_
  25.9 1.4 %collective-permute-start.11 = (bf16[1,48,2,512]{3,2,1,0:T(2,128)(2,1)S(1)}, bf16[1,48,2,512]{3,2,1,0:T(2,128)(2,1)S(1)}, u32[]{:S(2)}, u32[]{:S(2)}) collective-permute-start(bf16[1,48,2,512]{3,2,1,0:T(2,128)(2,1)S(1)} %get-tuple-element.42), channel_id=1, source_target_pairs={{0,1},{1,0},{2,3},{3,2},{4,5},{5,4},{6,7},{7,6},{8,9},{9,8},{10,11... | collective-permute-start | bytes 294920 | tf_op jit(solution)/shard_map/ppermute | solution.py:308
  27.3 0.8 %collective-permute-done.7.refs_6_ = bf16[1,48,2,512]{3,2,1,0:T(2,128)(2,1)S(1)} collective-permute-done((bf16[1,48,2,512]{3,2,1,0:T(2,128)(2,1)S(1)}, bf16[1,48,2,512]{3,2,1,0:T(2,128)(2,1)S(1)}, u32[]{:S(2)}, u32[]{:S(2)}) %collective-permute-start.7) | collective-permute-done | bytes 98336 | tf_op jit(solution)/shard_map/ppermute | solution.py:308
  28.1 5.5 %collective-permute-start.12 = (bf16[1,48,2,512]{3,2,1,0:T(2,128)(2,1)S(1)}, bf16[1,48,2,512]{3,2,1,0:T(2,128)(2,1)S(1)}, u32[]{:S(2)}, u32[]{:S(2)}) collective-permute-start(bf16[1,48,2,512]{3,2,1,0:T(2,128)(2,1)S(1)} %get-tuple-element.43), channel_id=1, source_target_pairs={{0,13},{1,7},{2,15},{3,5},{4,9},{5,3},{6,11},{7,1},{8,14},{9,4},{1... | collective-permute-start | bytes 294920 | tf_op jit(solution)/shard_map/ppermute | solution.py:308
  33.6 0.0 collective-permute-done.8.refs_7_
  33.6 0.0 collective-permute-start.13
  33.6 0.9 %collective-permute-done.9.refs_8_ = bf16[1,48,2,512]{3,2,1,0:T(2,128)(2,1)S(1)} collective-permute-done((bf16[1,48,2,512]{3,2,1,0:T(2,128)(2,1)S(1)}, bf16[1,48,2,512]{3,2,1,0:T(2,128)(2,1)S(1)}, u32[]{:S(2)}, u32[]{:S(2)}) %collective-permute-start.9) | collective-permute-done | bytes 98336 | tf_op jit(solution)/shard_map/ppermute | solution.py:308
  34.6 1.8 %collective-permute-start.14 = (bf16[1,48,2,512]{3,2,1,0:T(2,128)(2,1)S(1)}, bf16[1,48,2,512]{3,2,1,0:T(2,128)(2,1)S(1)}, u32[]{:S(2)}, u32[]{:S(2)}) collective-permute-start(bf16[1,48,2,512]{3,2,1,0:T(2,128)(2,1)S(1)} %get-tuple-element.45), channel_id=1, source_target_pairs={{0,14},{1,6},{2,12},{3,4},{4,3},{5,11},{6,1},{7,9},{8,15},{9,7},{1... | collective-permute-start | bytes 294920 | tf_op jit(solution)/shard_map/ppermute | solution.py:308
  36.4 0.0 collective-permute-done.10.refs_9_
  36.4 1.5 %collective-permute-start.15 = (bf16[1,48,2,512]{3,2,1,0:T(2,128)(2,1)S(1)}, bf16[1,48,2,512]{3,2,1,0:T(2,128)(2,1)S(1)}, u32[]{:S(2)}, u32[]{:S(2)}) collective-permute-start(bf16[1,48,2,512]{3,2,1,0:T(2,128)(2,1)S(1)} %get-tuple-element.46), channel_id=1, source_target_pairs={{0,7},{1,15},{2,5},{3,13},{4,10},{5,2},{6,8},{7,0},{8,6},{9,14},{1... | collective-permute-start | bytes 294920 | tf_op jit(solution)/shard_map/ppermute | solution.py:308
  37.9 0.0 collective-permute-done.11.refs_10_
  37.9 2.8 %collective-permute-start.16 = (bf16[1,48,2,512]{3,2,1,0:T(2,128)(2,1)S(1)}, bf16[1,48,2,512]{3,2,1,0:T(2,128)(2,1)S(1)}, u32[]{:S(2)}, u32[]{:S(2)}) collective-permute-start(bf16[1,48,2,512]{3,2,1,0:T(2,128)(2,1)S(1)} %get-tuple-element.48), channel_id=1, source_target_pairs={{0,15},{1,14},{2,13},{3,12},{4,11},{5,10},{6,9},{7,8},{8,7},{9,6},... | collective-permute-start | bytes 294920 | tf_op jit(solution)/shard_map/ppermute | solution.py:308
  40.7 1.7 %operators.1 = (bf16[512,256]{1,0:T(8,128)(2,1)S(1)}, bf16[256,256]{1,0:T(8,128)(2,1)S(1)}, bf16[1,48,2,512]{3,2,1,0:T(2,128)(2,1)S(1)}, f32[2,8,128]{2,1,0:T(8,128)S(1)}) custom-call(bf16[2,128,128]{2,1,0:T(8,128)(2,1)S(1)} %get-tuple-element.28.sink, bf16[2,128,128]{2,1,0:T(8,128)(2,1)S(1)} %get-tuple-element.29.source, ...), custom_call_target="tpu_custom_call" | custom-call | flops 100000000 | bytes 1000000 | tf_op jit(solution)/shard_map/operators/pallas_call | solution.py:55
  42.4 0.0 collective-permute-done.12.refs_11_
  42.4 0.0 collective-permute-done.13.refs_12_
  42.4 0.0 collective-permute-done.14.refs_13_
  42.4 4.1 %collective-permute-done.15.refs_14_ = bf16[1,48,2,512]{3,2,1,0:T(2,128)(2,1)S(1)} collective-permute-done((bf16[1,48,2,512]{3,2,1,0:T(2,128)(2,1)S(1)}, bf16[1,48,2,512]{3,2,1,0:T(2,128)(2,1)S(1)}, u32[]{:S(2)}, u32[]{:S(2)}) %collective-permute-start.15) | collective-permute-done | bytes 98336 | tf_op jit(solution)/shard_map/ppermute | solution.py:308
  46.5 1.6 %pack_early.1 = (bf16[4,512,2,128]{3,2,1,0:T(2,128)(2,1)S(1)}, f32[2,8,128]{2,1,0:T(8,128)S(1)}) custom-call(f32[2,8,128]{2,1,0:T(8,128)S(1)} %get-tuple-element.33.told_ref, bf16[1,48,2,512]{3,2,1,0:T(2,128)(2,1)S(1)} %get-tuple-element.34.refs_0_, bf16[1,48,2,512]{3,2,1,0:T(2,128)(2,1)S(1)} %collective-permute-done.2.refs_1_, ...), custom_call_target="tpu_custom_call" | custom-call | flops 100000000 | bytes 1000000 | tf_op jit(solution)/shard_map/pack_early/pallas_call | solution.py:194
  48.1 0.0 collective-permute-done.16.refs_0_
  48.2 3.2 %pair_loop.1 = (bf16[4,512,2,128]{3,2,1,0:T(2,128)(2,1)S(1)}, bf16[2,512,512]{2,1,0:T(8,128)(2,1)}) custom-call(bf16[512,256]{1,0:T(8,128)(2,1)S(1)} %get-tuple-element.31.f_ref, bf16[256,256]{1,0:T(8,128)(2,1)S(1)} %get-tuple-element.32.e_ref, f32[2,8,128]{2,1,0:T(8,128)S(1)} %get-tuple-element.47.late_ref, ...), custom_call_target="tpu_custom_call", output_to_operand_aliasing={{0}: (4, {})} | custom-call | flops 2000000000 | bytes 3000000 | tf_op jit(solution)/shard_map/pair_loop/pallas_call | solution.py:244
Async XLA Ops:
  1.1 19.5 %collective-permute-start.3 = (bf16[1,48,2,512]{3,2,1,0:T(2,128)(2,1)S(1)}, bf16[1,48,2,512]{3,2,1,0:T(2,128)(2,1)S(1)}, u32[]{:S(2)}, u32[]{:S(2)}) collective-permute-start(bf16[1,48,2,512]{3,2,1,0:T(2,128)(2,1)S(1)} %get-tuple-element.51), channel_id=1, source_target_pairs={{0,9},{1,3},{2,11},{3,1},{4,13},{5,7},{6,15},{7,5},{8,10},{9,0},{1... | collective-permute-start | bytes 294920 | tf_op jit(solution)/shard_map/ppermute | solution.py:308
  4.7 17.4 %collective-permute-start.2 = (bf16[1,48,2,512]{3,2,1,0:T(2,128)(2,1)S(1)}, bf16[1,48,2,512]{3,2,1,0:T(2,128)(2,1)S(1)}, u32[]{:S(2)}, u32[]{:S(2)}) collective-permute-start(bf16[1,48,2,512]{3,2,1,0:T(2,128)(2,1)S(1)} %get-tuple-element.52), channel_id=1, source_target_pairs={{0,8},{1,9},{2,10},{3,11},{4,12},{5,13},{6,14},{7,15},{8,0},{9,1},... | collective-permute-start | bytes 294920 | tf_op jit(solution)/shard_map/ppermute | solution.py:308
  9.4 15.1 %collective-permute-start.4 = (bf16[1,48,2,512]{3,2,1,0:T(2,128)(2,1)S(1)}, bf16[1,48,2,512]{3,2,1,0:T(2,128)(2,1)S(1)}, u32[]{:S(2)}, u32[]{:S(2)}) collective-permute-start(bf16[1,48,2,512]{3,2,1,0:T(2,128)(2,1)S(1)} %get-tuple-element.35), channel_id=1, source_target_pairs={{0,2},{1,8},{2,0},{3,10},{4,6},{5,12},{6,4},{7,14},{8,1},{9,11},{1... | collective-permute-start | bytes 294920 | tf_op jit(solution)/shard_map/ppermute | solution.py:308
  10.0 15.9 %collective-permute-start.5 = (bf16[1,48,2,512]{3,2,1,0:T(2,128)(2,1)S(1)}, bf16[1,48,2,512]{3,2,1,0:T(2,128)(2,1)S(1)}, u32[]{:S(2)}, u32[]{:S(2)}) collective-permute-start(bf16[1,48,2,512]{3,2,1,0:T(2,128)(2,1)S(1)} %get-tuple-element.36), channel_id=1, source_target_pairs={{0,10},{1,2},{2,1},{3,9},{4,14},{5,6},{6,5},{7,13},{8,11},{9,3},{1... | collective-permute-start | bytes 294920 | tf_op jit(solution)/shard_map/ppermute | solution.py:308
  11.6 4.3 %collective-permute-start.1 = (s32[1]{0:T(128)}, s32[1]{0:T(128)}, u32[]{:S(2)}, u32[]{:S(2)}) collective-permute-start(s32[1]{0:T(128)} %param.6), channel_id=1, source_target_pairs={{0,9},{1,3},{2,11},{3,1},{4,13},{5,7},{6,15},{7,5},{8,10},{9,0},{1... | collective-permute-start | bytes 20 | tf_op jit(solution)/shard_map/ppermute | solution.py:305
  15.9 4.7 %collective-permute-start = (s32[1]{0:T(128)}, s32[1]{0:T(128)}, u32[]{:S(2)}, u32[]{:S(2)}) collective-permute-start(s32[1]{0:T(128)} %param.6), channel_id=1, source_target_pairs={{0,8},{1,9},{2,10},{3,11},{4,12},{5,13},{6,14},{7,15},{8,0},{9,1},... | collective-permute-start | bytes 20 | tf_op jit(solution)/shard_map/ppermute | solution.py:305
  20.6 5.3 %collective-permute-start.6 = (bf16[1,48,2,512]{3,2,1,0:T(2,128)(2,1)S(1)}, bf16[1,48,2,512]{3,2,1,0:T(2,128)(2,1)S(1)}, u32[]{:S(2)}, u32[]{:S(2)}) collective-permute-start(bf16[1,48,2,512]{3,2,1,0:T(2,128)(2,1)S(1)} %get-tuple-element.37), channel_id=1, source_target_pairs={{0,3},{1,11},{2,8},{3,0},{4,7},{5,15},{6,12},{7,4},{8,2},{9,10},{1... | collective-permute-start | bytes 294920 | tf_op jit(solution)/shard_map/ppermute | solution.py:308
  20.6 7.5 %collective-permute-start.7 = (bf16[1,48,2,512]{3,2,1,0:T(2,128)(2,1)S(1)}, bf16[1,48,2,512]{3,2,1,0:T(2,128)(2,1)S(1)}, u32[]{:S(2)}, u32[]{:S(2)}) collective-permute-start(bf16[1,48,2,512]{3,2,1,0:T(2,128)(2,1)S(1)} %get-tuple-element.38), channel_id=1, source_target_pairs={{0,11},{1,5},{2,9},{3,7},{4,15},{5,1},{6,13},{7,3},{8,12},{9,2},{1... | collective-permute-start | bytes 294920 | tf_op jit(solution)/shard_map/ppermute | solution.py:308
  22.0 11.6 %collective-permute-start.8 = (bf16[1,48,2,512]{3,2,1,0:T(2,128)(2,1)S(1)}, bf16[1,48,2,512]{3,2,1,0:T(2,128)(2,1)S(1)}, u32[]{:S(2)}, u32[]{:S(2)}) collective-permute-start(bf16[1,48,2,512]{3,2,1,0:T(2,128)(2,1)S(1)} %get-tuple-element.39), channel_id=1, source_target_pairs={{0,4},{1,10},{2,6},{3,8},{4,0},{5,14},{6,2},{7,12},{8,3},{9,13},{1... | collective-permute-start | bytes 294920 | tf_op jit(solution)/shard_map/ppermute | solution.py:308
  24.5 10.1 %collective-permute-start.9 = (bf16[1,48,2,512]{3,2,1,0:T(2,128)(2,1)S(1)}, bf16[1,48,2,512]{3,2,1,0:T(2,128)(2,1)S(1)}, u32[]{:S(2)}, u32[]{:S(2)}) collective-permute-start(bf16[1,48,2,512]{3,2,1,0:T(2,128)(2,1)S(1)} %get-tuple-element.40), channel_id=1, source_target_pairs={{0,12},{1,4},{2,14},{3,6},{4,1},{5,9},{6,3},{7,11},{8,13},{9,5},{1... | collective-permute-start | bytes 294920 | tf_op jit(solution)/shard_map/ppermute | solution.py:308
  25.9 10.5 %collective-permute-start.10 = (bf16[1,48,2,512]{3,2,1,0:T(2,128)(2,1)S(1)}, bf16[1,48,2,512]{3,2,1,0:T(2,128)(2,1)S(1)}, u32[]{:S(2)}, u32[]{:S(2)}) collective-permute-start(bf16[1,48,2,512]{3,2,1,0:T(2,128)(2,1)S(1)} %get-tuple-element.41), channel_id=1, source_target_pairs={{0,5},{1,13},{2,7},{3,15},{4,8},{5,0},{6,10},{7,2},{8,4},{9,12},{1... | collective-permute-start | bytes 294920 | tf_op jit(solution)/shard_map/ppermute | solution.py:308
  25.9 12.0 %collective-permute-start.11 = (bf16[1,48,2,512]{3,2,1,0:T(2,128)(2,1)S(1)}, bf16[1,48,2,512]{3,2,1,0:T(2,128)(2,1)S(1)}, u32[]{:S(2)}, u32[]{:S(2)}) collective-permute-start(bf16[1,48,2,512]{3,2,1,0:T(2,128)(2,1)S(1)} %get-tuple-element.42), channel_id=1, source_target_pairs={{0,1},{1,0},{2,3},{3,2},{4,5},{5,4},{6,7},{7,6},{8,9},{9,8},{10,11... | collective-permute-start | bytes 294920 | tf_op jit(solution)/shard_map/ppermute | solution.py:308
  28.1 14.3 %collective-permute-start.12 = (bf16[1,48,2,512]{3,2,1,0:T(2,128)(2,1)S(1)}, bf16[1,48,2,512]{3,2,1,0:T(2,128)(2,1)S(1)}, u32[]{:S(2)}, u32[]{:S(2)}) collective-permute-start(bf16[1,48,2,512]{3,2,1,0:T(2,128)(2,1)S(1)} %get-tuple-element.43), channel_id=1, source_target_pairs={{0,13},{1,7},{2,15},{3,5},{4,9},{5,3},{6,11},{7,1},{8,14},{9,4},{1... | collective-permute-start | bytes 294920 | tf_op jit(solution)/shard_map/ppermute | solution.py:308
  33.6 8.8 %collective-permute-start.13 = (bf16[1,48,2,512]{3,2,1,0:T(2,128)(2,1)S(1)}, bf16[1,48,2,512]{3,2,1,0:T(2,128)(2,1)S(1)}, u32[]{:S(2)}, u32[]{:S(2)}) collective-permute-start(bf16[1,48,2,512]{3,2,1,0:T(2,128)(2,1)S(1)} %get-tuple-element.44), channel_id=1, source_target_pairs={{0,6},{1,12},{2,4},{3,14},{4,2},{5,8},{6,0},{7,10},{8,5},{9,15},{1... | collective-permute-start | bytes 294920 | tf_op jit(solution)/shard_map/ppermute | solution.py:308
  34.6 7.9 %collective-permute-start.14 = (bf16[1,48,2,512]{3,2,1,0:T(2,128)(2,1)S(1)}, bf16[1,48,2,512]{3,2,1,0:T(2,128)(2,1)S(1)}, u32[]{:S(2)}, u32[]{:S(2)}) collective-permute-start(bf16[1,48,2,512]{3,2,1,0:T(2,128)(2,1)S(1)} %get-tuple-element.45), channel_id=1, source_target_pairs={{0,14},{1,6},{2,12},{3,4},{4,3},{5,11},{6,1},{7,9},{8,15},{9,7},{1... | collective-permute-start | bytes 294920 | tf_op jit(solution)/shard_map/ppermute | solution.py:308
  36.4 10.1 %collective-permute-start.15 = (bf16[1,48,2,512]{3,2,1,0:T(2,128)(2,1)S(1)}, bf16[1,48,2,512]{3,2,1,0:T(2,128)(2,1)S(1)}, u32[]{:S(2)}, u32[]{:S(2)}) collective-permute-start(bf16[1,48,2,512]{3,2,1,0:T(2,128)(2,1)S(1)} %get-tuple-element.46), channel_id=1, source_target_pairs={{0,7},{1,15},{2,5},{3,13},{4,10},{5,2},{6,8},{7,0},{8,6},{9,14},{1... | collective-permute-start | bytes 294920 | tf_op jit(solution)/shard_map/ppermute | solution.py:308
  37.9 10.2 %collective-permute-start.16 = (bf16[1,48,2,512]{3,2,1,0:T(2,128)(2,1)S(1)}, bf16[1,48,2,512]{3,2,1,0:T(2,128)(2,1)S(1)}, u32[]{:S(2)}, u32[]{:S(2)}) collective-permute-start(bf16[1,48,2,512]{3,2,1,0:T(2,128)(2,1)S(1)} %get-tuple-element.48), channel_id=1, source_target_pairs={{0,15},{1,14},{2,13},{3,12},{4,11},{5,10},{6,9},{7,8},{8,7},{9,6},... | collective-permute-start | bytes 294920 | tf_op jit(solution)/shard_map/ppermute | solution.py:308
